TPU v7x, 128 devices: a whole 4x4x4 slice. The times are simulated.
128 devices in a mesh: slab: 32 (over y, z, x_lo), beam: 4 (over x_hi, core).
Axes of the slice: x: 4 (x_hi: 2, x_lo: 2; x = x_hi * 2 + x_lo), y: 4, z: 4, core: 2. Of those that a mesh axis runs over, the one named last changes fastest.
Arguments:
- traces: bfloat16 [2048, 128, 1024], P(('slab', 'beam')), may hold values from -6 to 6
- shot_window: int32 [2048], P(('slab', 'beam')), may hold values from 0 to 15, as said below
- trace_slot: int32 [2048, 128], P(('slab', 'beam')), may hold values from 0 to 63
- ray_phase: bfloat16 [256, 1024], replicated, may hold values from -0.1875 to 0.1875
- ray_index: int32 [16, 768], P('beam', 'slab'), may hold values from 0 to 255
- beam_basis: bfloat16 [2, 1024, 8192], P(None, 'beam'), may hold values from -0.125 to 0.125
Outputs:
- image: float32 [768, 8192], P('slab', 'beam')
Inputs may be any that keep to these rules, and one draw needn't show every extreme that they name: `shot_window`: within each aligned block of 16 shots (the shots of one device), for every beam owner b exactly 4 shots name a window w with w // 4 = b.
All inputs are finite; a program needn't handle non-finite values.
Results may differ from a plain program's by a relative error of at most 0.0041.
Values may be sent and summed in bfloat16 or wider, within the bound.
No kernel may reach another device: no remote copies, remote signals or barrier semaphores. Data moves between devices by JAX's collectives and lax.ppermute only.
A program may use at most 64 MiB of HBM per device.

v0:
```python
import math

import jax
import jax.numpy as jnp
from jax import lax
from jax.sharding import PartitionSpec as P

P_SIZE = 64
K = 64
WIN_OWN = 4


def slant_tables():
    phase_steps = (
        jnp.arange(P_SIZE, dtype=jnp.int32)[:, None] * jnp.arange(K, dtype=jnp.int32)[None, :] % K
    )
    angles = phase_steps.astype(jnp.float32) * jnp.float32(2.0 * math.pi / K)
    return (jnp.cos(angles), jnp.sin(angles))


def slant_stack(binned, cosine_table, sine_table):
    freq_count = binned.shape[-1] // 2
    real_part = binned[..., :freq_count]
    imag_part = binned[..., freq_count:]
    high = lax.Precision.HIGHEST
    panel_re = jnp.einsum("ps,wsf->wpf", cosine_table, real_part, precision=high) + jnp.einsum(
        "ps,wsf->wpf", sine_table, imag_part, precision=high
    )
    panel_im = jnp.einsum("ps,wsf->wpf", cosine_table, imag_part, precision=high) - jnp.einsum(
        "ps,wsf->wpf", sine_table, real_part, precision=high
    )
    return jnp.concatenate([panel_re, panel_im], axis=-1)


def bin_traces(samples, labels, wanted):
    binning = (wanted[:, None] == labels[None, :]).astype(jnp.bfloat16)
    return jnp.dot(binning, samples, preferred_element_type=jnp.float32)


def body(traces, shot_window, trace_slot, ray_phase, ray_index, beam_basis):
    shot_count, per_shot, doubled = traces.shape
    freq_count = doubled // 2
    beam_count = lax.axis_size("beam")
    slab_count = lax.axis_size("slab")
    stack_scale = (shot_count * slab_count * beam_count * per_shot / (WIN_OWN * beam_count)) ** (
        -0.5
    )
    cosine_table, sine_table = slant_tables()
    owners = shot_window // WIN_OWN
    matches = (owners[:, None] == jnp.arange(beam_count, dtype=jnp.int32)[None, :]).astype(
        jnp.int32
    )
    rank_in = jnp.sum(jnp.cumsum(matches, axis=0) * matches, axis=1) - 1
    target = owners * (shot_count // beam_count) + rank_in
    gather_order = (
        jnp.zeros((shot_count,), jnp.int32).at[target].set(jnp.arange(shot_count, dtype=jnp.int32))
    )
    local_labels = ((shot_window % WIN_OWN)[:, None] * K + trace_slot).astype(jnp.bfloat16)
    arrived, arrived_labels = (
        lax.all_to_all(traces[gather_order], "beam", split_axis=0, concat_axis=0, tiled=True),
        lax.all_to_all(local_labels[gather_order], "beam", split_axis=0, concat_axis=0, tiled=True),
    )
    labels = arrived_labels.astype(jnp.int32).reshape(-1)
    samples = arrived.reshape(-1, doubled)
    binned = bin_traces(samples, labels, jnp.arange(WIN_OWN * K, dtype=jnp.int32))
    partial_value = slant_stack(binned.reshape(WIN_OWN, K, doubled), cosine_table, sine_table)
    partial_value = partial_value.reshape(WIN_OWN * P_SIZE, doubled) * jnp.float32(stack_scale)
    beam_panel = lax.psum(partial_value, "slab").astype(jnp.bfloat16)
    ray_count = ray_phase.shape[0]
    depths = ray_index.shape[1]
    ray_pick = (
        ray_index.reshape(-1)[:, None] == jnp.arange(ray_count, dtype=jnp.int32)[None, :]
    ).astype(jnp.bfloat16)
    rays = jnp.dot(ray_pick, ray_phase, preferred_element_type=jnp.float32).astype(jnp.bfloat16)
    rays = rays.reshape(WIN_OWN, depths, doubled)
    panel_three = beam_panel.reshape(WIN_OWN, P_SIZE, doubled)
    panel_re = panel_three[..., :freq_count]
    panel_im = panel_three[..., freq_count:]
    left_re = jnp.concatenate([panel_re, -panel_im], axis=-1)
    left_im = jnp.concatenate([panel_im, panel_re], axis=-1)
    wave_re = jnp.einsum("wzf,wpf->zwp", rays, left_re, preferred_element_type=jnp.float32).astype(
        jnp.bfloat16
    )
    wave_im = jnp.einsum("wzf,wpf->zwp", rays, left_im, preferred_element_type=jnp.float32).astype(
        jnp.bfloat16
    )
    mixture = jnp.concatenate(
        [wave_re.reshape(depths, WIN_OWN * P_SIZE), -wave_im.reshape(depths, WIN_OWN * P_SIZE)],
        axis=1,
    )
    basis_rows = beam_basis.reshape(2 * WIN_OWN * P_SIZE, beam_basis.shape[2])
    image_part = jnp.dot(mixture, basis_rows, preferred_element_type=jnp.float32)
    return lax.psum_scatter(image_part, "beam", scatter_dimension=1, tiled=True)


def solution(mesh):
    in_specs = (
        P(("slab", "beam"), None, None),
        P(("slab", "beam")),
        P(("slab", "beam"), None),
        P(),
        P("beam", "slab"),
        P(None, "beam", None),
    )
    out_specs = P("slab", "beam")
    return jax.shard_map(body, mesh=mesh, in_specs=in_specs, out_specs=out_specs, check_vma=False)
```

profile of v0, /device:TPU:1, one launch (start us, length us, event | category | flops | bytes accessed | tf_op | source)
XLA Modules:
  0.0 295.8 jit_solution(17968223047291159660)
XLA Ops:
  6.5 0.0 copy-start
  6.5 0.7 fusion.43
  7.3 0.1 fusion.42
  7.4 0.2 select_reduce_fusion
  7.6 0.6 scatter_custom_fusion
  8.2 0.8 add_convert_fusion
  9.0 1.2 gather_fusion
  10.2 5.8 %all-to-all-start = ((bf16[4,4,128]{2,1,0:T(4,128)(2,1)}), bf16[4,4,128]{2,1,0:T(4,128)(2,1)S(1)}, u32[]{:S(2)}, u32[]{:S(2)}) async-start(bf16[4,4,128]{2,1,0:T(4,128)(2,1)} %bitcast), calls=%async_computation | async-start | bytes 8192 | tf_op jit(solution)/shard_map/all_to_all | solution.py:61
  15.9 5.0 %gather_fusion.1 = bf16[16,128,1024]{2,1,0:T(8,128)(2,1)} fusion(bf16[16,128,1024]{2,1,0:T(8,128)(2,1)} %param.6, s32[1024]{0:T(1024)S(1)} %pad_clamp_fusion), kind=kCustom, calls=%fused_computation.1 | custom fusion | bytes 8388672 | tf_op jit(solution)/shard_map/gather | solution.py:60
  20.9 0.0 copy-start.1
  20.9 0.0 all-to-all-done
  20.9 5.1 %all-to-all-start.1 = ((bf16[16,128,1024]{2,1,0:T(8,128)(2,1)}), bf16[16,128,1024]{2,1,0:T(8,128)(2,1)}, u32[]{:S(2)}, u32[]{:S(2)}) async-start(bf16[16,128,1024]{2,1,0:T(8,128)(2,1)} %gather_fusion.1), calls=%async_computation.1 | async-start | bytes 8388608 | tf_op jit(solution)/shard_map/all_to_all | solution.py:60
  26.1 0.0 reduce-scatter.2.cloned.1.call-start
  26.1 0.0 copy-done.1
  26.1 0.1 eq.65
  26.2 0.0 copy-done
  26.2 0.3 convolution_convert_fusion
  26.4 48.4 %all-to-all-done.1 = bf16[16,128,1024]{2,1,0:T(8,128)(2,1)} async-done(((bf16[16,128,1024]{2,1,0:T(8,128)(2,1)}), bf16[16,128,1024]{2,1,0:T(8,128)(2,1)}, u32[]{:S(2)}, u32[]{:S(2)}) %all-to-all-start.1) | async-done | bytes 4194336 | tf_op jit(solution)/shard_map/all_to_all | solution.py:60
  74.8 3.5 %fusion = f32[4,64,1024]{2,1,0:T(8,128)S(1)} fusion(bf16[2048,1024,1]{1,0,2:T(8,128)(2,1)} %bitcast.3, s32[2048]{0:T(1024)S(1)} %convert.1, s32[4,64]{1,0:T(4,128)S(1)} %multiply_add_fusion), kind=kOutput, calls=%fused_computation.3 | convolution fusion | flops 1074266112 | bytes 5252096 | tf_op jit(solution)/shard_map/dot_general | solution.py:37
  78.3 0.8 fusion.19
  79.1 0.8 fusion.15
  79.9 0.8 fusion.3
  80.6 0.8 fusion.2
  81.4 0.1 maximum_multiply_fusion
  81.5 149.0 %all-reduce.1 = bf16[256,1024]{1,0:T(8,128)(2,1)S(1)} all-reduce(f32[256,1024]{1,0:T(8,128)S(1)} %bitcast.34), channel_id=1, replica_groups=mesh['slab'=32,'beam'=4] {'slab'}, use_global_device_ids=true, to_apply=%region_3.4 | all-reduce | flops 262144 | bytes 1572864 | tf_op jit(solution)/shard_map/psum | solution.py:68
  230.5 0.1 slice_negate_fusion
  230.6 0.2 fusion.4
  230.8 0.1 reshape.55
  230.9 0.2 fusion.6
  231.2 0.1 neg.15
  231.3 5.5 %fusion.32 = f32[24,8192]{1,0:T(8,128)} fusion(bf16[512,8192]{1,0:T(8,128)(2,1)} %bitcast.33, bf16[24,256]{1,0:T(8,128)(2,1)S(1)} %neg.15, bf16[24,256]{1,0:T(8,128)(2,1)S(1)} %reshape.55), kind=kOutput, calls=%fused_computation.45 | convolution fusion | flops 201375744 | bytes 9199616 | tf_op jit(solution)/shard_map/dot_general | solution.py:92
  236.8 0.0 reduce-scatter.2.cloned.1.call-update
  236.8 52.1 %reduce-scatter.2.cloned.1.call-done = f32[24,2048]{1,0:T(8,128)} async-done(((f32[24,8192]{1,0:T(8,128)}), f32[24,2048]{1,0:T(8,128)}) %reduce-scatter.2.cloned.1.call-update) | async-done | bytes 196624 | tf_op jit(solution)/shard_map/reduce_scatter | solution.py:93
  (9 shorter events, 0.1 us)
Async XLA Ops:
  6.5 19.6 %copy-start = (bf16[256,1024]{1,0:T(8,128)(2,1)S(1)}, bf16[256,1024]{1,0:T(8,128)(2,1)}, u32[]{:S(2)}) copy-start(bf16[256,1024]{1,0:T(8,128)(2,1)} %param.9) | copy-start | bytes 1572868
  10.2 10.8 %all-to-all-start = ((bf16[4,4,128]{2,1,0:T(4,128)(2,1)}), bf16[4,4,128]{2,1,0:T(4,128)(2,1)S(1)}, u32[]{:S(2)}, u32[]{:S(2)}) async-start(bf16[4,4,128]{2,1,0:T(4,128)(2,1)} %bitcast), calls=%async_computation | async-start | bytes 8192 | tf_op jit(solution)/shard_map/all_to_all | solution.py:61
  20.9 5.1 %copy-start.1 = (s32[4,24]{1,0:T(4,128)S(1)}, s32[4,24]{1,0:T(4,128)}, u32[]{:S(2)}) copy-start(s32[4,24]{1,0:T(4,128)} %param.10) | copy-start | bytes 1156
  20.9 53.9 %all-to-all-start.1 = ((bf16[16,128,1024]{2,1,0:T(8,128)(2,1)}), bf16[16,128,1024]{2,1,0:T(8,128)(2,1)}, u32[]{:S(2)}, u32[]{:S(2)}) async-start(bf16[16,128,1024]{2,1,0:T(8,128)(2,1)} %gather_fusion.1), calls=%async_computation.1 | async-start | bytes 8388608 | tf_op jit(solution)/shard_map/all_to_all | solution.py:60
  26.1 262.9 %reduce-scatter.2.cloned.1.call-start = ((), (), s32[]{:S(2)}) async-start(), calls=%async_computation.3 | async-start | bytes 983040 | tf_op jit(solution)/shard_map/reduce_scatter | solution.py:93
Sparse Core Ops, SparseCore 0:
  236.9 51.9 reduce-scatter.1
where the time goes:
time: 296 us
  blocking collectives  149 us (50%)
  waiting for transfers between devices  101 us (34%)
  between operations  13.5 us (5%)
  matrix products  12.8 us (4%)
  starting transfers between devices  10.9 us (4%)
  local copies, waits for them, and re-layouts  7.07 us (2%)
    psum x1, blocking collectives, body(): beam_panel = lax.psum(partial_value, 'slab').astype(jnp.bfloat16)  149 us
    reduce_scatter x1, waiting for transfers between devices, body(): return lax.psum_scatter(image_part, 'beam', scatter_dimension=1, tiled=True)  52.1 us
    all_to_all x1, waiting for transfers between devices, body(): lax.all_to_all(traces[gather_order], 'beam', split_axis=0, concat_axis=0,...  48.4 us
  transfers between devices with their start and end apart: 3, of which 2 were waited for; matrix products, arithmetic and copies ran while one was open for 2% of the time, Pallas kernels for 0%

commit v1 on v0

v1 whole, which is shorter than its diff:
```python
import functools
import math

import jax
import jax.numpy as jnp
import numpy as np
from jax import lax
from jax.experimental import pallas as pl
from jax.experimental.pallas import tpu as pltpu
from jax.sharding import PartitionSpec as P

P_SIZE = 64
K = 64
WIN_OWN = 4
AXES = ("slab", "beam")
BF16 = jnp.bfloat16
F32 = jnp.float32


def slant_table(scale):
    steps = np.arange(P_SIZE)[:, None] * np.arange(K)[None, :] % K
    angles = steps * (2.0 * math.pi / K)
    c, d = np.cos(angles) * scale, np.sin(angles) * scale
    full = np.stack([np.concatenate([c, d]), np.concatenate([d, -c])])
    full = full.astype(np.float32)
    high = full.astype(BF16)
    low = (full - high.astype(np.float32)).astype(BF16)
    table = np.concatenate([high[0], low[0], high[1], low[1]], axis=0)
    return np.pad(table, ((0, 0), (0, 128 - K)))


def split(value):
    high = value.astype(BF16)
    return high, (value - high.astype(F32)).astype(BF16)


def ray_weights(ray_ref, weight_ref):
    rays, doubled = ray_ref.shape
    half = doubled // 2
    weight_ref[:rays, :half] = ray_ref[:, :half]
    weight_ref[:rays, half:] = -ray_ref[:, half:]
    weight_ref[rays:, :half] = ray_ref[:, half:]
    weight_ref[rays:, half:] = ray_ref[:, :half]


NT = (((1,), (1,)), ((), ()))


def stack_kernel(group, window_ref, slot_ref, table_ref, ray_ref, trace_ref, out_ref, weight_ref, acc_ref):
    step = pl.program_id(0)
    rays = ray_ref.shape[0]
    per_shot = trace_ref.shape[1]

    @pl.when(step == 0)
    def _():
        ray_weights(ray_ref, weight_ref)
        acc_ref[...] = jnp.zeros_like(acc_ref)

    samples = trace_ref[...].reshape(group * per_shot, trace_ref.shape[2])
    value = lax.dot_general(samples, weight_ref[...], NT, preferred_element_type=F32)
    high, low = split(value)
    slot_rows = lax.broadcasted_iota(jnp.int32, (128, per_shot), 0)
    for j in range(group):
        shot = step * group + j
        slots = slot_ref[pl.ds(shot, 1), :]
        pick = (slot_rows == slots).astype(F32).astype(BF16)
        factors = jnp.dot(table_ref[...], pick, preferred_element_type=F32).astype(BF16)
        factors = jnp.concatenate([factors[:256], factors[256:]], axis=1)
        rows = slice(j * per_shot, (j + 1) * per_shot)
        right_high = jnp.concatenate([high[rows, :rays], high[rows, rays:]], axis=0)
        right_low = jnp.concatenate([low[rows, :rays], low[rows, rays:]], axis=0)
        one = jnp.dot(factors, right_high, preferred_element_type=F32)
        two = jnp.dot(factors[:128], right_low, preferred_element_type=F32)
        window = window_ref[shot]
        acc_ref[window] += one[:128] + one[128:] + two

    @pl.when(step == pl.num_programs(0) - 1)
    def _():
        for b in range(4):
            for wl in range(WIN_OWN):
                for h in range(2):
                    block = acc_ref[b * WIN_OWN + wl, h * 64 : (h + 1) * 64, :].astype(BF16)
                    first = h * 16 + wl * 4
                    out_ref[first : first + 4, b] = block.reshape(4, 16, rays)


def stack(window, slots, table, ray_phase, traces):
    shots, per_shot, doubled = traces.shape
    rays = ray_phase.shape[0]
    group = 4
    whole = lambda shape: pl.BlockSpec(shape, lambda i, w: (0,) * len(shape))
    return pl.pallas_call(
        functools.partial(stack_kernel, group),
        out_shape=jax.ShapeDtypeStruct((32, 4, 16, rays), BF16),
        grid_spec=pltpu.PrefetchScalarGridSpec(
            num_scalar_prefetch=1,
            grid=(shots // group,),
            in_specs=[
                whole(slots.shape),
                whole(table.shape),
                whole(ray_phase.shape),
                pl.BlockSpec((group, per_shot, doubled), lambda i, w: (i, 0, 0)),
            ],
            out_specs=whole((32, 4, 16, rays)),
            scratch_shapes=[
                pltpu.VMEM((2 * rays, doubled), BF16),
                pltpu.VMEM((16, 2 * P_SIZE, rays), F32),
            ],
        ),
        compiler_params=pltpu.CompilerParams(vmem_limit_bytes=32 << 20),
        name="stack",
    )(window, slots, table, ray_phase, traces)


def image_kernel(index_ref, ray_ref, basis_ref, out_ref, left_ref):
    @pl.when(pl.program_id(0) == 0)
    def _():
        rays = ray_ref.shape[-1]
        depths = index_ref.shape[0] // WIN_OWN
        lanes = lax.broadcasted_iota(jnp.int32, (WIN_OWN * depths, rays), 1)
        index = jnp.concatenate([index_ref[...], index_ref[...]], axis=1)
        pick = (lanes == index).astype(F32).astype(BF16)
        group = lax.broadcasted_iota(jnp.int32, (depths, 512), 1) // P_SIZE % WIN_OWN
        for part in range(2):
            table = ray_ref[:, part].reshape(512, rays)
            waves = lax.dot_general(pick, table, NT, preferred_element_type=F32)
            wave = waves[:depths]
            for wl in range(1, WIN_OWN):
                wave = jnp.where(group == wl, waves[wl * depths : (wl + 1) * depths], wave)
            left_ref[part * depths : (part + 1) * depths, :] = wave

    depths = out_ref.shape[1]
    basis = basis_ref[...].reshape(512, basis_ref.shape[2])
    terms = jnp.dot(left_ref[...].astype(BF16), basis, preferred_element_type=F32)
    out_ref[0] = (terms[:depths] + terms[depths:]).astype(BF16)


def image(index, rays, basis):
    depths = index.shape[0] // WIN_OWN
    laterals = basis.shape[2]
    tile = 1024
    per = laterals // 4 // tile
    whole = lambda shape: pl.BlockSpec(shape, lambda i: (0,) * len(shape))
    return pl.pallas_call(
        image_kernel,
        out_shape=jax.ShapeDtypeStruct((4, depths, laterals // 4), BF16),
        grid=(laterals // tile,),
        in_specs=[
            whole(index.shape),
            whole(rays.shape),
            pl.BlockSpec((2, 256, tile), lambda i: (0, 0, i)),
        ],
        out_specs=pl.BlockSpec((1, depths, tile), lambda i: (i // per, 0, i % per)),
        scratch_shapes=[pltpu.VMEM((2 * depths, 512), F32)],
        compiler_params=pltpu.CompilerParams(vmem_limit_bytes=32 << 20),
        name="image",
    )(index, rays, basis)


def body(traces, shot_window, trace_slot, ray_phase, ray_index, beam_basis):
    shots, per_shot, doubled = traces.shape
    rays = ray_phase.shape[0]
    depths = ray_index.shape[1]
    devices = lax.axis_size("slab") * lax.axis_size("beam")
    scale = (shots * devices * per_shot / (WIN_OWN * lax.axis_size("beam"))) ** -0.5
    index = jnp.broadcast_to(ray_index.reshape(WIN_OWN * depths, 1), (WIN_OWN * depths, 128))
    part = stack(shot_window, trace_slot, slant_table(scale), ray_phase, traces)
    arrived = lax.all_to_all(part.reshape(devices, 16, rays), AXES, 0, 0, tiled=True)
    mine = jnp.sum(arrived.astype(F32), axis=0)
    pair = jnp.stack(split(mine))
    sent = jnp.broadcast_to(pair[None], (32, 2, 16, rays))
    table = lax.all_to_all(sent, "slab", 0, 0, tiled=True)
    terms = image(index, table, beam_basis)
    arrived = lax.all_to_all(terms, "beam", 0, 0, tiled=True)
    return jnp.sum(arrived.astype(F32), axis=0)


def solution(mesh):
    in_specs = (
        P(("slab", "beam"), None, None),
        P(("slab", "beam")),
        P(("slab", "beam"), None),
        P(),
        P("beam", "slab"),
        P(None, "beam", None),
    )
    return jax.shard_map(
        body, mesh=mesh, in_specs=in_specs, out_specs=P("slab", "beam"), check_vma=False
    )
```

time: 296 us -> 79 us (0.27)
  blocking collectives: 149 us -> 42.7 us
  waiting for transfers between devices: 101 us -> 11.1 us
  between operations: 13.5 us -> 0.05 us
  matrix products: 12.8 us -> 0 us
  Pallas kernels: 0 us -> 9.99 us
  starting transfers between devices: 10.9 us -> 3.89 us
    psum x1 -> x0, blocking collectives: 149 us -> none  [body(): beam_panel = lax.psum(partial_value, 'slab').astype(jnp.bfloat16)]
    reduce_scatter x1 -> x0, waiting for transfers between devices: 52.1 us -> none  [body(): return lax.psum_scatter(image_part, 'beam', scatter_dimension=1, tiled=True)]
    all_to_all x0 -> x2, blocking collectives: none -> 42.7 us  [the longest x1 30.4 us: body(): lax.all_to_all(part.reshape(devices, 16, rays), AXES, 0, 0, tiled=True)]
    all_to_all x2 -> x1, waiting for transfers between devices: 48.4 us -> 11.1 us  [body(): table = lax.all_to_all(sent, 'slab', 0, 0, tiled=True)]
    dot_general x9 -> x0, matrix products: 12.8 us -> none  [the longest x1 5.47 us: body(): jnp.dot(mixture, basis_rows, preferred_element_type=jnp.float32)]
    pallas_call x0 -> x2, Pallas kernels: none -> 9.99 us  [the longest x1 6.49 us: stack(): pl.pallas_call(functools.partial(stack_kernel, group), out_shape=jax.Shap...]
    unnamed x4 -> x14, local copies, waits for them, and re-layouts: 0.01 us -> 8.88 us
    all_to_all x2 -> x1, starting transfers between devices: 10.9 us -> 3.89 us  [body(): table = lax.all_to_all(sent, 'slab', 0, 0, tiled=True)]
  transfers between devices with their start and end apart: 3 -> 1, of which waited for: 2 -> 1; matrix products, arithmetic and copies ran while one was open for 2% -> 0% of each run, Pallas kernels for 0% -> 0%
where the time goes in v1:
time: 79 us; the launch traced here: 78.5 us
  blocking collectives  42.7 us (54%)
  waiting for transfers between devices  11.1 us (14%)
  Pallas kernels  9.99 us (13%)
  local copies, waits for them, and re-layouts  9.89 us (13%)
  starting transfers between devices  3.89 us (5%)
  other arithmetic  0.93 us (1%)
    all_to_all x1, blocking collectives, body(): lax.all_to_all(part.reshape(devices, 16, rays), AXES, 0, 0, tiled=True)  30.4 us
    all_to_all x1, blocking collectives, body(): arrived = lax.all_to_all(terms, 'beam', 0, 0, tiled=True)  12.4 us
    all_to_all x1, waiting for transfers between devices, body(): table = lax.all_to_all(sent, 'slab', 0, 0, tiled=True)  11.1 us
    unnamed x14, local copies, waits for them, and re-layouts  8.88 us
    pallas_call x1, Pallas kernels, stack(): pl.pallas_call(functools.partial(stack_kernel, group), out_shape=jax.Shap...  6.49 us
    all_to_all x1, starting transfers between devices, body(): table = lax.all_to_all(sent, 'slab', 0, 0, tiled=True)  3.89 us
    pallas_call x1, Pallas kernels, image(): pl.pallas_call(image_kernel, out_shape=jax.ShapeDtypeStruct((4, depths, l...  3.49 us
  transfers between devices with their start and end apart: 1, of which 1 were waited for; matrix products, arithmetic and copies ran while one was open for 0% of the time, Pallas kernels for 0%

profile of v1, /device:TPU:1, one launch (start us, length us, event | category | flops | bytes accessed | tf_op | source)
XLA Modules:
  0.0 78.5 jit_solution(5308641815830578114)
XLA Ops:
  0.0 0.0 copy-start.1
  0.0 2.2 %copy-done.1 = bf16[16,128,1024]{2,1,0:T(8,128)(2,1)S(1)} copy-done((bf16[16,128,1024]{2,1,0:T(8,128)(2,1)S(1)}, bf16[16,128,1024]{2,1,0:T(8,128)(2,1)}, u32[]{:S(2)}) %copy-start.1) | copy-done | bytes 4194328
  2.2 0.0 copy-start.2
  2.2 1.0 %copy-done.2 = bf16[256,1024]{1,0:T(8,128)(2,1)S(1)} copy-done((bf16[256,1024]{1,0:T(8,128)(2,1)S(1)}, bf16[256,1024]{1,0:T(8,128)(2,1)}, u32[]{:S(2)}) %copy-start.2) | copy-done | bytes 524312
  3.2 0.0 copy-start.3
  3.2 0.9 %copy-done.3 = bf16[512,128]{1,0:T(8,128)(2,1)S(1)} copy-done((bf16[512,128]{1,0:T(8,128)(2,1)S(1)}, bf16[512,128]{1,0:T(8,128)(2,1)}, u32[]{:S(2)}) %copy-start.3) | copy-done | bytes 131096
  4.1 0.0 copy-start.4
  4.1 0.7 copy-done.4
  4.8 0.0 copy-start.5
  4.8 0.7 copy-done.5
  5.5 0.0 copy-start.6
  5.5 6.5 %stack.7 = bf16[32,4,16,256]{3,2,1,0:T(8,128)(2,1)S(1)} custom-call(s32[16]{0:T(128)S(1)} %copy-done.5, s32[16,128]{1,0:T(8,128)S(1)} %copy-done.4, bf16[512,128]{1,0:T(8,128)(2,1)S(1)} %copy-done.3, bf16[256,1024]{1,0:T(8,128)(2,1)S(1)} %copy-done.2, bf16[16,128,1024]{2,1,0:T(8,128)(2,1)S(1)} %copy-done.1), custom_call_target="tpu_custom_call" | custom-call | tf_op jit(solution)/shard_map/stack/pallas_call | solution.py:92
  12.0 30.4 %all_to_all.15 = bf16[128,16,256]{2,1,0:T(8,128)(2,1)S(1)} all-to-all(bf16[128,16,256]{2,1,0:T(8,128)(2,1)S(1)} %bitcast.7), channel_id=1, replica_groups=mesh['slab'=32,'beam'=4] {'slab','beam'}, dimensions={0} | all-to-all | bytes 2097152 | tf_op jit(solution)/shard_map/all_to_all | solution.py:168
  42.4 0.2 convert_reduce_fusion
  42.6 0.9 %broadcast_in_dim.15 = bf16[32,2,16,256]{3,2,1,0:T(8,128)(2,1)} broadcast(bf16[2,16,256]{2,1,0:T(8,128)(2,1)S(1)} %pad_maximum_fusion), dimensions={1,2,3} | broadcast | bytes 540672 | tf_op jit(solution)/shard_map/broadcast_in_dim | solution.py:171
  43.4 3.9 %all-to-all-start.1 = ((bf16[32,2,16,256]{3,2,1,0:T(8,128)(2,1)}), bf16[32,2,16,256]{3,2,1,0:T(8,128)(2,1)S(1)}, u32[]{:S(2)}, u32[]{:S(2)}) async-start(bf16[32,2,16,256]{3,2,1,0:T(8,128)(2,1)} %broadcast_in_dim.15), calls=%async_computation.1 | async-start | bytes 1048576 | tf_op jit(solution)/shard_map/all_to_all | solution.py:172
  47.3 0.0 copy-done.6
  47.3 0.1 broadcast_in_dim.6
  47.4 11.1 %all-to-all-done.1.ray_ref = bf16[32,2,16,256]{3,2,1,0:T(8,128)(2,1)S(1)} async-done(((bf16[32,2,16,256]{3,2,1,0:T(8,128)(2,1)}), bf16[32,2,16,256]{3,2,1,0:T(8,128)(2,1)S(1)}, u32[]{:S(2)}, u32[]{:S(2)}) %all-to-all-start.1) | async-done | bytes 524320 | tf_op jit(solution)/shard_map/all_to_all | solution.py:172
  58.5 0.1 broadcast_in_dim.14.index_ref
  58.6 0.0 copy-start
  58.6 3.4 %copy-done = bf16[2,256,8192]{2,1,0:T(8,128)(2,1)S(1)} copy-done((bf16[2,256,8192]{2,1,0:T(8,128)(2,1)S(1)}, bf16[2,256,8192]{2,1,0:T(8,128)(2,1)}, u32[]{:S(2)}) %copy-start) | copy-done | bytes 8388632
  62.0 3.5 %image.1 = bf16[4,24,2048]{2,1,0:T(8,128)(2,1)S(1)} custom-call(s32[96,128]{1,0:T(8,128)S(1)} %broadcast_in_dim.14.index_ref, bf16[32,2,16,256]{3,2,1,0:T(8,128)(2,1)S(1)} %all-to-all-done.1.ray_ref, bf16[2,256,8192]{2,1,0:T(8,128)(2,1)S(1)} %copy-done), custom_call_target="tpu_custom_call" | custom-call | tf_op jit(solution)/shard_map/image/pallas_call | solution.py:144
  65.5 12.4 %all_to_all.16 = bf16[4,24,2048]{2,1,0:T(8,128)(2,1)S(1)} all-to-all(bf16[4,24,2048]{2,1,0:T(8,128)(2,1)S(1)} %image.1), channel_id=1, replica_groups=mesh['slab'=32,'beam'=4] {'beam'}, dimensions={0} | all-to-all | bytes 786432 | tf_op jit(solution)/shard_map/all_to_all | solution.py:174
  77.8 0.7 convert_reduce_fusion.1
  (2 shorter events, 0.0 us)
Async XLA Ops:
  0.0 2.2 %copy-start.1 = (bf16[16,128,1024]{2,1,0:T(8,128)(2,1)S(1)}, bf16[16,128,1024]{2,1,0:T(8,128)(2,1)}, u32[]{:S(2)}) copy-start(bf16[16,128,1024]{2,1,0:T(8,128)(2,1)} %trace_ref.1) | copy-start | bytes 12582916
  2.2 1.0 %copy-start.2 = (bf16[256,1024]{1,0:T(8,128)(2,1)S(1)}, bf16[256,1024]{1,0:T(8,128)(2,1)}, u32[]{:S(2)}) copy-start(bf16[256,1024]{1,0:T(8,128)(2,1)} %ray_ref.1) | copy-start | bytes 1572868
  3.2 0.9 %copy-start.3 = (bf16[512,128]{1,0:T(8,128)(2,1)S(1)}, bf16[512,128]{1,0:T(8,128)(2,1)}, u32[]{:S(2)}) copy-start(bf16[512,128]{1,0:T(8,128)(2,1)} %constant.4.clone.table_ref) | copy-start | bytes 393220
  4.1 0.7 copy-start.4
  4.8 0.7 copy-start.5
  5.5 41.9 %copy-start.6 = (s32[4,24]{1,0:T(4,128)S(1)}, s32[4,24]{1,0:T(4,128)}, u32[]{:S(2)}) copy-start(s32[4,24]{1,0:T(4,128)} %param.11) | copy-start | bytes 1156
  43.4 15.1 %all-to-all-start.1 = ((bf16[32,2,16,256]{3,2,1,0:T(8,128)(2,1)}), bf16[32,2,16,256]{3,2,1,0:T(8,128)(2,1)S(1)}, u32[]{:S(2)}, u32[]{:S(2)}) async-start(bf16[32,2,16,256]{3,2,1,0:T(8,128)(2,1)} %broadcast_in_dim.15), calls=%async_computation.1 | async-start | bytes 1048576 | tf_op jit(solution)/shard_map/all_to_all | solution.py:172
  58.6 3.4 %copy-start = (bf16[2,256,8192]{2,1,0:T(8,128)(2,1)S(1)}, bf16[2,256,8192]{2,1,0:T(8,128)(2,1)}, u32[]{:S(2)}) copy-start(bf16[2,256,8192]{2,1,0:T(8,128)(2,1)} %basis_ref.1) | copy-start | bytes 25165828

commit v2 on v1

v2 whole, which is shorter than its diff:
```python
import functools
import math

import jax
import jax.numpy as jnp
import numpy as np
from jax import lax
from jax.experimental import pallas as pl
from jax.experimental.pallas import tpu as pltpu
from jax.sharding import PartitionSpec as P


P_SIZE = 64
K = 64
WIN_OWN = 4
AXES = ("slab", "beam")
BF16 = jnp.bfloat16
F32 = jnp.float32
NT = (((1,), (1,)), ((), ()))
HBM = pl.BlockSpec(memory_space=pltpu.HBM)
VMEM = pl.BlockSpec(memory_space=pltpu.VMEM)


def slant_table(scale):
    steps = np.arange(P_SIZE)[:, None] * np.arange(K)[None, :] % K
    angles = steps * (2.0 * math.pi / K)
    full = (np.concatenate([np.cos(angles), np.sin(angles)]) * scale).astype(np.float32)
    high = full.astype(BF16)
    low = (full - high.astype(np.float32)).astype(BF16)
    return np.pad(np.concatenate([high, low]), ((0, 0), (0, 128 - K)))


def split(value):
    high = value.astype(BF16)
    return high, (value - high.astype(F32)).astype(BF16)


def beam_position():
    position = lax.axis_index("beam")
    return lax.div(position, 2), lax.rem(position, 2)


def stack_kernel(
    group, window_hbm, slot_hbm, table_hbm, ray_hbm, trace_hbm, mine_ref, other_ref,
    buffer, window_ref, slot_ref, table_ref, ray_ref, weight_ref, acc_ref, sems, trace_sems,
):
    rays, doubled = ray_ref.shape
    half = doubled // 2
    shots, per_shot, _ = trace_hbm.shape
    pairs = ((window_hbm, window_ref), (ray_hbm, ray_ref), (slot_hbm, slot_ref), (table_hbm, table_ref))
    small = [pltpu.make_async_copy(a, b, sems.at[i]) for i, (a, b) in enumerate(pairs)]
    loads = []
    for g in range(shots // group):
        part = pl.ds(g * group, group)
        loads.append(pltpu.make_async_copy(trace_hbm.at[part], buffer.at[part], trace_sems.at[g]))
    for copy in small + loads:
        copy.start()
    _, core = beam_position()
    acc_ref[...] = jnp.zeros_like(acc_ref)
    small[1].wait()
    weight_ref[:rays, :half] = ray_ref[:, :half]
    weight_ref[:rays, half:] = -ray_ref[:, half:]
    weight_ref[rays:, :half] = ray_ref[:, half:]
    weight_ref[rays:, half:] = ray_ref[:, :half]
    for copy in (small[0], small[2], small[3]):
        copy.wait()
    slot_rows = lax.broadcasted_iota(jnp.int32, (128, per_shot), 0)
    for g in range(shots // group):
        first = g * group
        factors = []
        for j in range(0, group, 2):
            picks = []
            for shot in (first + j, first + j + 1):
                slots = slot_ref[shot : shot + 1, :]
                picks.append((slot_rows == slots).astype(F32).astype(BF16))
            both = jnp.dot(
                table_ref[...], jnp.concatenate(picks, axis=1), preferred_element_type=F32
            ).astype(BF16)
            for i in range(2):
                left = both[:, i * per_shot : (i + 1) * per_shot]
                right = jnp.concatenate(
                    [left[64:128], -left[:64], left[192:], -left[128:192]], axis=0
                )
                factors.append(jnp.concatenate([left, right], axis=1))
        loads[g].wait()
        samples = buffer[first : first + group].reshape(group * per_shot, doubled)
        value = lax.dot_general(samples, weight_ref[...], NT, preferred_element_type=F32)
        high, low = split(value)
        for j in range(group):
            rows = slice(j * per_shot, (j + 1) * per_shot)
            right_high = jnp.concatenate([high[rows, :rays], high[rows, rays:]], axis=0)
            right_low = jnp.concatenate([low[rows, :rays], low[rows, rays:]], axis=0)
            one = jnp.dot(factors[j], right_high, preferred_element_type=F32)
            two = jnp.dot(factors[j][:128], right_low, preferred_element_type=F32)
            window = window_ref[first + j]
            away = ((window >> 2) & 1) ^ core
            acc_ref[away * 8 + (window >> 3) * 4 + (window & 3)] += one[:128] + one[128:] + two
    for side in range(2):
        for wl in range(WIN_OWN):
            for h in range(2):
                at = h * 16 + wl * 4
                rows = slice(h * 64, (h + 1) * 64)
                block = acc_ref[side * 4 + wl, rows]
                mine_ref[at : at + 4, side] = block.reshape(4, 16, rays)
                block = acc_ref[8 + side * 4 + wl, rows].astype(other_ref.dtype)
                other_ref[at : at + 4, side] = block.reshape(4, 16, rays)


def stack(window, slots, table, ray_phase, traces):
    shots, _, doubled = traces.shape
    rays = ray_phase.shape[0]
    group = 4
    return pl.pallas_call(
        functools.partial(stack_kernel, group),
        out_shape=(
            jax.ShapeDtypeStruct((32, 2, 16, rays), F32),
            jax.ShapeDtypeStruct((32, 2, 16, rays), BF16),
        ),
        in_specs=[HBM] * 5,
        out_specs=(VMEM, VMEM),
        scratch_shapes=[
            pltpu.VMEM(traces.shape, BF16),
            pltpu.SMEM(window.shape, jnp.int32),
            pltpu.VMEM(slots.shape, jnp.int32),
            pltpu.VMEM(table.shape, BF16),
            pltpu.VMEM(ray_phase.shape, BF16),
            pltpu.VMEM((2 * rays, doubled), BF16),
            pltpu.VMEM((16, 2 * P_SIZE, rays), F32),
            pltpu.SemaphoreType.DMA((4,)),
            pltpu.SemaphoreType.DMA((shots // group,)),
        ],
        compiler_params=pltpu.CompilerParams(vmem_limit_bytes=STACK_VMEM),
        name="stack",
    )(window, slots, table, ray_phase, traces)


STACK_VMEM = 61 << 20
IMAGE_VMEM = 57 << 20


def spread_kernel(arrived_ref, out_ref):
    total = jnp.sum(arrived_ref[...].astype(F32), axis=0).astype(out_ref.dtype)
    for i in range(out_ref.shape[0]):
        out_ref[i] = total


def spread(arrived):
    return pl.pallas_call(
        spread_kernel,
        out_shape=jax.ShapeDtypeStruct((32,) + arrived.shape[1:], BF16),
        in_specs=[VMEM],
        out_specs=VMEM,
        name="spread",
    )(arrived)


def select(index_ref, table_ref, lane_ref):
    rays = table_ref.shape[-1]
    depths = index_ref.shape[1]
    lane_ref[:WIN_OWN, :depths] = index_ref[...]
    spread_out = lane_ref[...]
    lane = lax.broadcasted_iota(jnp.int32, (1, 128), 1)
    index = jnp.zeros((1, 128), jnp.int32)
    for wl in range(WIN_OWN):
        moved = pltpu.roll(spread_out, wl * depths, 1)[wl : wl + 1]
        here = (lane >= wl * depths) & (lane < (wl + 1) * depths)
        index = jnp.where(here, moved, index)
    rows = lax.broadcasted_iota(jnp.int32, (rays, 128), 0)
    pick = jnp.transpose((rows == index).astype(F32)).astype(BF16)
    group = lax.broadcasted_iota(jnp.int32, (depths, 512), 1) // P_SIZE % WIN_OWN
    table = table_ref[...].reshape(512, rays)
    waves = lax.dot_general(pick, table, NT, preferred_element_type=F32)
    wave = waves[:depths]
    for wl in range(1, WIN_OWN):
        wave = jnp.where(group == wl, waves[wl * depths : (wl + 1) * depths], wave)
    return wave.astype(BF16)


PIECES = 4


def basis_loads(far, other, basis_hbm, basis_ref, sems):
    side, core = beam_position()
    chunk = (1 - side if far else side) * 2 + (1 - core if other else core)
    width = basis_ref.shape[2] // PIECES
    loads = []
    for i in range(PIECES):
        source = pl.ds(pl.multiple_of(chunk * basis_ref.shape[2] + i * width, width), width)
        target = pl.ds(i * width, width)
        loads.append(
            pltpu.make_async_copy(
                basis_hbm.at[:, :, source], basis_ref.at[:, :, target], sems.at[i]
            )
        )
        loads[-1].start()
    return loads


def multiply(wave, loads, basis_ref, out_ref):
    width = basis_ref.shape[2] // PIECES
    for i, load in enumerate(loads):
        load.wait()
        columns = slice(i * width, (i + 1) * width)
        basis = basis_ref[:, :, columns].reshape(512, width)
        out_ref[:, columns] = jnp.dot(wave, basis, preferred_element_type=F32)


def first_kernel(index_ref, table_ref, basis_hbm, out_ref, wave_ref, basis_ref, sems, lane_ref):
    loads = basis_loads(True, True, basis_hbm, basis_ref, sems)
    wave_ref[...] = select(index_ref, table_ref, lane_ref)
    multiply(wave_ref[...], loads, basis_ref, out_ref)


def later_kernel(far, other, wave_ref, basis_hbm, out_ref, basis_ref, sems):
    loads = basis_loads(far, other, basis_hbm, basis_ref, sems)
    multiply(wave_ref[...], loads, basis_ref, out_ref)


def image_call(kernel, depths, laterals, basis, wave_out, *operands):
    shape = jax.ShapeDtypeStruct((depths, laterals), F32)
    wave = jax.ShapeDtypeStruct((depths, 512), BF16)
    return pl.pallas_call(
        kernel,
        out_shape=(shape, wave) if wave_out else shape,
        in_specs=[VMEM] * len(operands) + [HBM],
        out_specs=(VMEM, VMEM) if wave_out else VMEM,
        scratch_shapes=[
            pltpu.VMEM((2, 256, laterals), BF16),
            pltpu.SemaphoreType.DMA((PIECES,)),
        ]
        + [pltpu.VMEM((8, 128), jnp.int32)] * wave_out,
        compiler_params=pltpu.CompilerParams(vmem_limit_bytes=IMAGE_VMEM),
        cost_estimate=pl.CostEstimate(
            flops=2 * depths * 512 * laterals, bytes_accessed=1024 * laterals, transcendentals=0
        ),
    )(*operands, basis)


def body(traces, shot_window, trace_slot, ray_phase, ray_index, beam_basis):
    shots, per_shot, _ = traces.shape
    rays = ray_phase.shape[0]
    depths = ray_index.shape[1]
    slabs, beams = lax.axis_size("slab"), lax.axis_size("beam")
    devices = slabs * beams
    chunk = beam_basis.shape[2] // beams
    scale = (shots * devices * per_shot / (WIN_OWN * beams)) ** -0.5
    partner = [(i, i ^ 1) for i in range(devices)]
    distant = [(i, i ^ 2) for i in range(devices)]
    same_core = [list(range(core, devices, 2)) for core in range(2)]

    mine, other = stack(shot_window, trace_slot, slant_table(scale), ray_phase, traces)
    other = lax.ppermute(other, AXES, partner)
    both = (mine + other.astype(F32)).astype(BF16).reshape(2 * slabs, 16, rays)
    arrived = lax.all_to_all(both, AXES, 0, 0, axis_index_groups=same_core, tiled=True)
    table = lax.all_to_all(spread(arrived), "slab", 0, 0, tiled=True)

    far_other, wave = image_call(first_kernel, depths, chunk, beam_basis, True, ray_index, table)
    call = lambda far, other, wave: image_call(
        functools.partial(later_kernel, far, other), depths, chunk, beam_basis, False, wave
    )
    far_other = lax.ppermute(far_other, AXES, partner)
    far_mine = call(True, False, wave)
    far = (far_mine + far_other).astype(BF16)
    far = lax.ppermute(far, AXES, distant)
    near_other = call(False, True, wave)
    near_other = lax.ppermute(near_other, AXES, partner)
    near_mine = call(False, False, wave)
    return near_mine + near_other + far.astype(F32)


def solution(mesh):
    in_specs = (
        P(("slab", "beam"), None, None),
        P(("slab", "beam")),
        P(("slab", "beam"), None),
        P(),
        P("beam", "slab"),
        P(None, "beam", None),
    )
    return jax.shard_map(
        body, mesh=mesh, in_specs=in_specs, out_specs=P("slab", "beam"), check_vma=False
    )
```

time: 79 us -> 72.7 us (0.920)
  Pallas kernels: 9.99 us -> 23 us
  local copies, waits for them, and re-layouts: 9.89 us -> 0 us
  waiting for transfers between devices: 11.1 us -> 2.67 us
  blocking collectives: 42.7 us -> 36.6 us
  other arithmetic: 0.93 us -> 3.97 us
  starting transfers between devices: 3.89 us -> 5.74 us
    pallas_call x2 -> x6, Pallas kernels: 9.99 us -> 23 us  [the longest x4 13.4 us: image_call(): pl.pallas_call(kernel, out_shape=(shape, wave) if wave_out else shape, in...]
    all_to_all x1 -> x0, waiting for transfers between devices: 11.1 us -> none  [body(): table = lax.all_to_all(sent, 'slab', 0, 0, tiled=True)]
    unnamed x14 -> x0, local copies, waits for them, and re-layouts: 8.88 us -> none
    all_to_all x2, blocking collectives: 42.7 us -> 36.6 us  [the longest x1 23.7 us: body(): lax.all_to_all(both, AXES, 0, 0, axis_index_groups=same_core, tiled=True)]
    ppermute x0 -> x4, starting transfers between devices: none -> 5.74 us  [the longest x1 2.98 us: body(): far_other = lax.ppermute(far_other, AXES, partner)]
    all_to_all x1 -> x0, starting transfers between devices: 3.89 us -> none  [body(): table = lax.all_to_all(sent, 'slab', 0, 0, tiled=True)]
    ppermute x0 -> x4, waiting for transfers between devices: none -> 2.67 us  [the longest x1 1.75 us: body(): other = lax.ppermute(other, AXES, partner)]
    convert_element_type x1 -> x2, other arithmetic: 0.01 us -> 2.34 us  [the longest x1 1.39 us: body(): both = (mine + other.astype(F32)).astype(BF16).reshape(2 * slabs, 16, rays)]
  transfers between devices with their start and end apart: 1 -> 4, of which waited for: 1 -> 2; matrix products, arithmetic and copies ran while one was open for 0% -> 1% of each run, Pallas kernels for 0% -> 14%
where the time goes in v2:
time: 72.7 us; the launch traced here: 72 us
  blocking collectives  36.6 us (50%)
  Pallas kernels  23 us (32%)
  starting transfers between devices  5.74 us (8%)
  other arithmetic  3.97 us (5%)
  waiting for transfers between devices  2.67 us (4%)
    all_to_all x1, blocking collectives, body(): lax.all_to_all(both, AXES, 0, 0, axis_index_groups=same_core, tiled=True)  23.7 us
    pallas_call x4, Pallas kernels, image_call(): pl.pallas_call(kernel, out_shape=(shape, wave) if wave_out else shape, in...  13.4 us
    all_to_all x1, blocking collectives, body(): table = lax.all_to_all(spread(arrived), 'slab', 0, 0, tiled=True)  12.9 us
    pallas_call x1, Pallas kernels, stack(): pl.pallas_call(functools.partial(stack_kernel, group), out_shape=(jax.Sha...  7.76 us
    ppermute x1, starting transfers between devices, body(): far_other = lax.ppermute(far_other, AXES, partner)  2.98 us
    pallas_call x1, Pallas kernels, spread(): pl.pallas_call(spread_kernel, out_shape=jax.ShapeDtypeStruct((32,) + arri...  1.83 us
    ppermute x1, waiting for transfers between devices, body(): other = lax.ppermute(other, AXES, partner)  1.75 us
    add x1, other arithmetic, body(): return near_mine + near_other + far.astype(F32)  1.63 us
  transfers between devices with their start and end apart: 4, of which 2 were waited for; matrix products, arithmetic and copies ran while one was open for 1% of the time, Pallas kernels for 14%

profile of v2, /device:TPU:1, one launch (start us, length us, event | category | flops | bytes accessed | tf_op | source)
XLA Modules:
  0.0 72.0 jit_solution(14239817805093666118)
XLA Ops:
  0.0 7.8 %stack.1 = (f32[32,2,16,256]{3,2,1,0:T(8,128)}, bf16[32,2,16,256]{3,2,1,0:T(8,128)(2,1)}) custom-call(s32[16]{0:T(128)} %window_hbm.1, s32[16,128]{1,0:T(8,128)} %slot_hbm.1, bf16[256,128]{1,0:T(8,128)(2,1)} %constant.2.clone.table_hbm, bf16[256,1024]{1,0:T(8,128)(2,1)} %ray_hbm.1, bf16[16,128,1024]{2,1,0:T(8,128)(2,1)} %trace_hbm.1), custom_call_target="tpu_custom_call" | custom-call | tf_op jit(solution)/shard_map/stack/pallas_call | solution.py:113
  7.8 1.5 %collective-permute-start = (bf16[32,2,16,256]{3,2,1,0:T(8,128)(2,1)}, bf16[32,2,16,256]{3,2,1,0:T(8,128)(2,1)S(1)}, u32[]{:S(2)}, u32[]{:S(2)}) collective-permute-start(bf16[32,2,16,256]{3,2,1,0:T(8,128)(2,1)} %get-tuple-element.10), channel_id=1, source_target_pairs={{0,1},{1,0},{2,3},{3,2},{4,5},{5,4},{6,7},{7,6},{8,9},{9,8},{10,11... | collective-permute-start | bytes 1572872 | tf_op jit(solution)/shard_map/ppermute | solution.py:252
  9.2 1.7 %collective-permute-done = bf16[32,2,16,256]{3,2,1,0:T(8,128)(2,1)S(1)} collective-permute-done((bf16[32,2,16,256]{3,2,1,0:T(8,128)(2,1)}, bf16[32,2,16,256]{3,2,1,0:T(8,128)(2,1)S(1)}, u32[]{:S(2)}, u32[]{:S(2)}) %collective-permute-start) | collective-permute-done | bytes 524320 | tf_op jit(solution)/shard_map/ppermute | solution.py:252
  11.0 1.4 %add_convert_fusion = bf16[32,2,16,256]{3,2,1,0:T(8,128)(2,1)S(1)} fusion(f32[32,2,16,256]{3,2,1,0:T(8,128)} %get-tuple-element.9, bf16[32,2,16,256]{3,2,1,0:T(8,128)(2,1)S(1)} %collective-permute-done), kind=kLoop, calls=%fused_computation | loop fusion | flops 786432 | bytes 2097152 | tf_op jit(solution)/shard_map/convert_element_type | solution.py:253
  12.4 23.7 %all_to_all.10.arrived_ref = bf16[64,16,256]{2,1,0:T(8,128)(2,1)} all-to-all(bf16[64,16,256]{2,1,0:T(8,128)(2,1)S(1)} %bitcast.1), channel_id=1, replica_groups={{0,2,4,6,8,10,12,14,16,18,20,22,24,26,28,30,32,34,36,38,40,42,44,46,48,..., dimensions={0} | all-to-all | bytes 1048576 | tf_op jit(solution)/shard_map/all_to_all | solution.py:254
  36.1 1.8 %spread.1 = bf16[32,16,256]{2,1,0:T(8,128)(2,1)} custom-call(bf16[64,16,256]{2,1,0:T(8,128)(2,1)} %all_to_all.10.arrived_ref), custom_call_target="tpu_custom_call" | custom-call | tf_op jit(solution)/shard_map/spread/pallas_call | solution.py:148
  37.9 12.9 %all_to_all.11.table_ref = bf16[32,16,256]{2,1,0:T(8,128)(2,1)} all-to-all(bf16[32,16,256]{2,1,0:T(8,128)(2,1)} %spread.1), channel_id=1, replica_groups=mesh['slab'=32,'beam'=4] {'slab'}, dimensions={0} | all-to-all | bytes 524288 | tf_op jit(solution)/shard_map/all_to_all | solution.py:255
  50.8 3.5 %shard_map.73 = (f32[24,2048]{1,0:T(8,128)}, bf16[24,512]{1,0:T(8,128)(2,1)}) custom-call(s32[4,24]{1,0:T(4,128)} %index_ref.1, bf16[32,16,256]{2,1,0:T(8,128)(2,1)} %all_to_all.11.table_ref, bf16[2,256,8192]{2,1,0:T(8,128)(2,1)} %basis_hbm.7), custom_call_target="tpu_custom_call" | custom-call | flops 50331648 | bytes 2097152 | tf_op jit(solution)/shard_map/pallas_call | solution.py:222
  54.3 3.0 %collective-permute-start.2 = (f32[24,2048]{1,0:T(8,128)}, f32[24,2048]{1,0:T(8,128)S(1)}, u32[]{:S(2)}, u32[]{:S(2)}) collective-permute-start(f32[24,2048]{1,0:T(8,128)} %get-tuple-element.12), channel_id=1, source_target_pairs={{0,1},{1,0},{2,3},{3,2},{4,5},{5,4},{6,7},{7,6},{8,9},{9,8},{10,11... | collective-permute-start | bytes 589832 | tf_op jit(solution)/shard_map/ppermute | solution.py:261
  57.3 3.3 %shard_map.75 = f32[24,2048]{1,0:T(8,128)} custom-call(bf16[24,512]{1,0:T(8,128)(2,1)} %get-tuple-element.11.wave_ref, bf16[2,256,8192]{2,1,0:T(8,128)(2,1)} %basis_hbm.7), custom_call_target="tpu_custom_call" | custom-call | flops 50331648 | bytes 2097152 | tf_op jit(solution)/shard_map/pallas_call | solution.py:222
  60.6 0.1 collective-permute-start.1
  60.7 3.3 %shard_map.76 = f32[24,2048]{1,0:T(8,128)} custom-call(bf16[24,512]{1,0:T(8,128)(2,1)} %get-tuple-element.11.wave_ref, bf16[2,256,8192]{2,1,0:T(8,128)(2,1)} %basis_hbm.7), custom_call_target="tpu_custom_call" | custom-call | flops 50331648 | bytes 2097152 | tf_op jit(solution)/shard_map/pallas_call | solution.py:222
  64.0 0.0 collective-permute-done.2
  64.0 0.9 %add_convert_fusion.1 = bf16[24,2048]{1,0:T(8,128)(2,1)S(1)} fusion(f32[24,2048]{1,0:T(8,128)} %shard_map.76, f32[24,2048]{1,0:T(8,128)S(1)} %collective-permute-done.2), kind=kLoop, calls=%fused_computation.2 | loop fusion | flops 98304 | bytes 491520 | tf_op jit(solution)/shard_map/convert_element_type | solution.py:263
  64.9 1.2 %collective-permute-start.3 = (bf16[24,2048]{1,0:T(8,128)(2,1)S(1)}, bf16[24,2048]{1,0:T(8,128)(2,1)S(1)}, u32[]{:S(2)}, u32[]{:S(2)}) collective-permute-start(bf16[24,2048]{1,0:T(8,128)(2,1)S(1)} %add_convert_fusion.1), channel_id=1, source_target_pairs={{0,2},{1,3},{2,0},{3,1},{4,6},{5,7},{6,4},{7,5},{8,10},{9,11},{10,... | collective-permute-start | bytes 294920 | tf_op jit(solution)/shard_map/ppermute | solution.py:264
  66.2 3.3 %shard_map.74 = f32[24,2048]{1,0:T(8,128)} custom-call(bf16[24,512]{1,0:T(8,128)(2,1)} %get-tuple-element.11.wave_ref, bf16[2,256,8192]{2,1,0:T(8,128)(2,1)} %basis_hbm.7), custom_call_target="tpu_custom_call" | custom-call | flops 50331648 | bytes 2097152 | tf_op jit(solution)/shard_map/pallas_call | solution.py:222
  69.5 0.0 collective-permute-done.1
  69.5 0.9 %collective-permute-done.3 = bf16[24,2048]{1,0:T(8,128)(2,1)S(1)} collective-permute-done((bf16[24,2048]{1,0:T(8,128)(2,1)S(1)}, bf16[24,2048]{1,0:T(8,128)(2,1)S(1)}, u32[]{:S(2)}, u32[]{:S(2)}) %collective-permute-start.3) | collective-permute-done | bytes 98336 | tf_op jit(solution)/shard_map/ppermute | solution.py:264
  70.4 1.6 %convert_add_fusion = f32[24,2048]{1,0:T(8,128)} fusion(bf16[24,2048]{1,0:T(8,128)(2,1)S(1)} %collective-permute-done.3, f32[24,2048]{1,0:T(8,128)} %shard_map.74, f32[24,2048]{1,0:T(8,128)S(1)} %collective-permute-done.1), kind=kLoop, calls=%fused_computation.1 | loop fusion | flops 147456 | bytes 688128 | tf_op jit(solution)/shard_map/add | solution.py:268
Async XLA Ops:
  7.8 3.2 %collective-permute-start = (bf16[32,2,16,256]{3,2,1,0:T(8,128)(2,1)}, bf16[32,2,16,256]{3,2,1,0:T(8,128)(2,1)S(1)}, u32[]{:S(2)}, u32[]{:S(2)}) collective-permute-start(bf16[32,2,16,256]{3,2,1,0:T(8,128)(2,1)} %get-tuple-element.10), channel_id=1, source_target_pairs={{0,1},{1,0},{2,3},{3,2},{4,5},{5,4},{6,7},{7,6},{8,9},{9,8},{10,11... | collective-permute-start | bytes 1572872 | tf_op jit(solution)/shard_map/ppermute | solution.py:252
  54.3 9.7 %collective-permute-start.2 = (f32[24,2048]{1,0:T(8,128)}, f32[24,2048]{1,0:T(8,128)S(1)}, u32[]{:S(2)}, u32[]{:S(2)}) collective-permute-start(f32[24,2048]{1,0:T(8,128)} %get-tuple-element.12), channel_id=1, source_target_pairs={{0,1},{1,0},{2,3},{3,2},{4,5},{5,4},{6,7},{7,6},{8,9},{9,8},{10,11... | collective-permute-start | bytes 589832 | tf_op jit(solution)/shard_map/ppermute | solution.py:261
  60.6 8.9 %collective-permute-start.1 = (f32[24,2048]{1,0:T(8,128)}, f32[24,2048]{1,0:T(8,128)S(1)}, u32[]{:S(2)}, u32[]{:S(2)}) collective-permute-start(f32[24,2048]{1,0:T(8,128)} %shard_map.75), channel_id=1, source_target_pairs={{0,1},{1,0},{2,3},{3,2},{4,5},{5,4},{6,7},{7,6},{8,9},{9,8},{10,11... | collective-permute-start | bytes 589832 | tf_op jit(solution)/shard_map/ppermute | solution.py:266
  64.9 5.4 %collective-permute-start.3 = (bf16[24,2048]{1,0:T(8,128)(2,1)S(1)}, bf16[24,2048]{1,0:T(8,128)(2,1)S(1)}, u32[]{:S(2)}, u32[]{:S(2)}) collective-permute-start(bf16[24,2048]{1,0:T(8,128)(2,1)S(1)} %add_convert_fusion.1), channel_id=1, source_target_pairs={{0,2},{1,3},{2,0},{3,1},{4,6},{5,7},{6,4},{7,5},{8,10},{9,11},{10,... | collective-permute-start | bytes 294920 | tf_op jit(solution)/shard_map/ppermute | solution.py:264

commit v3 on v2

--- a/solution.py
+++ b/solution.py
@@ -134,8 +134,8 @@
     )(window, slots, table, ray_phase, traces)
 
 
-STACK_VMEM = 61 << 20
-IMAGE_VMEM = 57 << 20
+STACK_VMEM = 54 << 20
+IMAGE_VMEM = 12 << 20
 
 
 def spread_kernel(arrived_ref, out_ref):
@@ -150,6 +150,7 @@
         out_shape=jax.ShapeDtypeStruct((32,) + arrived.shape[1:], BF16),
         in_specs=[VMEM],
         out_specs=VMEM,
+        compiler_params=pltpu.CompilerParams(vmem_limit_bytes=8 << 20),
         name="spread",
     )(arrived)
 
@@ -176,44 +177,26 @@
     return wave.astype(BF16)
 
 
-PIECES = 4
-
-
-def basis_loads(far, other, basis_hbm, basis_ref, sems):
+def multiply(far, other, wave, basis_ref, out_ref):
     side, core = beam_position()
     chunk = (1 - side if far else side) * 2 + (1 - core if other else core)
-    width = basis_ref.shape[2] // PIECES
-    loads = []
-    for i in range(PIECES):
-        source = pl.ds(pl.multiple_of(chunk * basis_ref.shape[2] + i * width, width), width)
-        target = pl.ds(i * width, width)
-        loads.append(
-            pltpu.make_async_copy(
-                basis_hbm.at[:, :, source], basis_ref.at[:, :, target], sems.at[i]
-            )
+    laterals = out_ref.shape[1]
+    width = 512
+    for i in range(laterals // width):
+        columns = pl.ds(pl.multiple_of(chunk * laterals + i * width, width), width)
+        basis = basis_ref[:, :, columns].reshape(512, width)
+        out_ref[:, i * width : (i + 1) * width] = jnp.dot(
+            wave, basis, preferred_element_type=F32
         )
-        loads[-1].start()
-    return loads
-
-
-def multiply(wave, loads, basis_ref, out_ref):
-    width = basis_ref.shape[2] // PIECES
-    for i, load in enumerate(loads):
-        load.wait()
-        columns = slice(i * width, (i + 1) * width)
-        basis = basis_ref[:, :, columns].reshape(512, width)
-        out_ref[:, columns] = jnp.dot(wave, basis, preferred_element_type=F32)
-
-
-def first_kernel(index_ref, table_ref, basis_hbm, out_ref, wave_ref, basis_ref, sems, lane_ref):
-    loads = basis_loads(True, True, basis_hbm, basis_ref, sems)
+
+
+def first_kernel(index_ref, table_ref, basis_ref, out_ref, wave_ref, lane_ref):
     wave_ref[...] = select(index_ref, table_ref, lane_ref)
-    multiply(wave_ref[...], loads, basis_ref, out_ref)
-
-
-def later_kernel(far, other, wave_ref, basis_hbm, out_ref, basis_ref, sems):
-    loads = basis_loads(far, other, basis_hbm, basis_ref, sems)
-    multiply(wave_ref[...], loads, basis_ref, out_ref)
+    multiply(True, True, wave_ref[...], basis_ref, out_ref)
+
+
+def later_kernel(far, other, wave_ref, basis_ref, out_ref):
+    multiply(far, other, wave_ref[...], basis_ref, out_ref)
 
 
 def image_call(kernel, depths, laterals, basis, wave_out, *operands):
@@ -222,13 +205,9 @@
     return pl.pallas_call(
         kernel,
         out_shape=(shape, wave) if wave_out else shape,
-        in_specs=[VMEM] * len(operands) + [HBM],
+        in_specs=[VMEM] * (len(operands) + 1),
         out_specs=(VMEM, VMEM) if wave_out else VMEM,
-        scratch_shapes=[
-            pltpu.VMEM((2, 256, laterals), BF16),
-            pltpu.SemaphoreType.DMA((PIECES,)),
-        ]
-        + [pltpu.VMEM((8, 128), jnp.int32)] * wave_out,
+        scratch_shapes=[pltpu.VMEM((8, 128), jnp.int32)] * wave_out,
         compiler_params=pltpu.CompilerParams(vmem_limit_bytes=IMAGE_VMEM),
         cost_estimate=pl.CostEstimate(
             flops=2 * depths * 512 * laterals, bytes_accessed=1024 * laterals, transcendentals=0

time: 72.7 us -> 59.1 us (0.81)
  Pallas kernels: 23 us -> 10.1 us
  waiting for transfers between devices: 2.67 us -> 4.79 us
  other arithmetic: 3.97 us -> 2.12 us
  blocking collectives: 36.6 us -> 34.9 us
  starting transfers between devices: 5.74 us -> 6.91 us
    pallas_call x4, Pallas kernels: 13.4 us -> 2.1 us  [image_call(): pl.pallas_call(kernel, out_shape=(shape, wave) if wave_out else shape, in...]
    ppermute x1, waiting for transfers between devices: 0.92 us -> 2.93 us  [body(): far = lax.ppermute(far, AXES, distant)]
    pallas_call x1, Pallas kernels: 1.83 us -> 0.1 us  [spread(): pl.pallas_call(spread_kernel, out_shape=jax.ShapeDtypeStruct((32,) + arri...]
    all_to_all x1, blocking collectives: 12.9 us -> 11.3 us  [body(): table = lax.all_to_all(spread(arrived), 'slab', 0, 0, tiled=True)]
    ppermute x1, starting transfers between devices: 1.21 us -> 2.16 us  [body(): far = lax.ppermute(far, AXES, distant)]
    convert_element_type x1, other arithmetic: 0.95 us -> 0.02 us  [body(): far = (far_mine + far_other).astype(BF16)]
    add x1, other arithmetic: 1.63 us -> 0.7 us  [body(): return near_mine + near_other + far.astype(F32)]
  transfers between devices with their start and end apart: 4 -> 4, of which waited for: 2 -> 3; matrix products, arithmetic and copies ran while one was open for 1% -> 0% of each run, Pallas kernels for 14% -> 2%
where the time goes in v3:
time: 59.1 us; the launch traced here: 58.8 us
  blocking collectives  34.9 us (59%)
  Pallas kernels  10.1 us (17%)
  starting transfers between devices  6.91 us (12%)
  waiting for transfers between devices  4.79 us (8%)
  other arithmetic  2.12 us (4%)
    all_to_all x1, blocking collectives, body(): lax.all_to_all(both, AXES, 0, 0, axis_index_groups=same_core, tiled=True)  23.6 us
    all_to_all x1, blocking collectives, body(): table = lax.all_to_all(spread(arrived), 'slab', 0, 0, tiled=True)  11.3 us
    pallas_call x1, Pallas kernels, stack(): pl.pallas_call(functools.partial(stack_kernel, group), out_shape=(jax.Sha...  7.91 us
    ppermute x1, starting transfers between devices, body(): far_other = lax.ppermute(far_other, AXES, partner)  3.25 us
    ppermute x1, waiting for transfers between devices, body(): far = lax.ppermute(far, AXES, distant)  2.93 us
    ppermute x1, starting transfers between devices, body(): far = lax.ppermute(far, AXES, distant)  2.16 us
    pallas_call x4, Pallas kernels, image_call(): pl.pallas_call(kernel, out_shape=(shape, wave) if wave_out else shape, in...  2.1 us
    ppermute x1, waiting for transfers between devices, body(): other = lax.ppermute(other, AXES, partner)  1.75 us
  transfers between devices with their start and end apart: 4, of which 3 were waited for; matrix products, arithmetic and copies ran while one was open for 0% of the time, Pallas kernels for 2%

profile of v3, /device:TPU:1, one launch (start us, length us, event | category | flops | bytes accessed | tf_op | source)
XLA Modules:
  0.0 58.8 jit_solution(14062648831250655463)
XLA Ops:
  0.0 0.0 copy-start
  0.0 0.0 copy-start.1
  0.0 7.9 %stack.1 = (f32[32,2,16,256]{3,2,1,0:T(8,128)}, bf16[32,2,16,256]{3,2,1,0:T(8,128)(2,1)}) custom-call(s32[16]{0:T(128)} %window_hbm.1, s32[16,128]{1,0:T(8,128)} %slot_hbm.1, bf16[256,128]{1,0:T(8,128)(2,1)} %constant.2.clone.table_hbm, bf16[256,1024]{1,0:T(8,128)(2,1)} %ray_hbm.1, bf16[16,128,1024]{2,1,0:T(8,128)(2,1)} %trace_hbm.1), custom_call_target="tpu_custom_call" | custom-call | tf_op jit(solution)/shard_map/stack/pallas_call | solution.py:113
  7.9 1.5 %collective-permute-start = (bf16[32,2,16,256]{3,2,1,0:T(8,128)(2,1)}, bf16[32,2,16,256]{3,2,1,0:T(8,128)(2,1)S(1)}, u32[]{:S(2)}, u32[]{:S(2)}) collective-permute-start(bf16[32,2,16,256]{3,2,1,0:T(8,128)(2,1)} %get-tuple-element.10), channel_id=1, source_target_pairs={{0,1},{1,0},{2,3},{3,2},{4,5},{5,4},{6,7},{7,6},{8,9},{9,8},{10,11... | collective-permute-start | bytes 1572872 | tf_op jit(solution)/shard_map/ppermute | solution.py:231
  9.4 1.7 %collective-permute-done = bf16[32,2,16,256]{3,2,1,0:T(8,128)(2,1)S(1)} collective-permute-done((bf16[32,2,16,256]{3,2,1,0:T(8,128)(2,1)}, bf16[32,2,16,256]{3,2,1,0:T(8,128)(2,1)S(1)}, u32[]{:S(2)}, u32[]{:S(2)}) %collective-permute-start) | collective-permute-done | bytes 524320 | tf_op jit(solution)/shard_map/ppermute | solution.py:231
  11.1 1.4 %add_convert_fusion = bf16[32,2,16,256]{3,2,1,0:T(8,128)(2,1)S(1)} fusion(f32[32,2,16,256]{3,2,1,0:T(8,128)} %get-tuple-element.9, bf16[32,2,16,256]{3,2,1,0:T(8,128)(2,1)S(1)} %collective-permute-done), kind=kLoop, calls=%fused_computation | loop fusion | flops 786432 | bytes 2097152 | tf_op jit(solution)/shard_map/convert_element_type | solution.py:232
  12.5 23.6 %all_to_all.10.arrived_ref = bf16[64,16,256]{2,1,0:T(8,128)(2,1)S(1)} all-to-all(bf16[64,16,256]{2,1,0:T(8,128)(2,1)S(1)} %bitcast.1), channel_id=1, replica_groups={{0,2,4,6,8,10,12,14,16,18,20,22,24,26,28,30,32,34,36,38,40,42,44,46,48,..., dimensions={0} | all-to-all | bytes 1048576 | tf_op jit(solution)/shard_map/all_to_all | solution.py:233
  36.1 0.1 spread.1
  36.2 11.3 %all_to_all.11.table_ref = bf16[32,16,256]{2,1,0:T(8,128)(2,1)S(1)} all-to-all(bf16[32,16,256]{2,1,0:T(8,128)(2,1)S(1)} %spread.1), channel_id=1, replica_groups=mesh['slab'=32,'beam'=4] {'slab'}, dimensions={0} | all-to-all | bytes 524288 | tf_op jit(solution)/shard_map/all_to_all | solution.py:234
  47.5 0.0 copy-done
  47.5 0.0 copy-done.1
  47.5 0.7 %shard_map.73 = (f32[24,2048]{1,0:T(8,128)S(1)}, bf16[24,512]{1,0:T(8,128)(2,1)S(1)}) custom-call(s32[4,24]{1,0:T(4,128)S(1)} %copy-done.1, bf16[32,16,256]{2,1,0:T(8,128)(2,1)S(1)} %all_to_all.11.table_ref, bf16[2,256,8192]{2,1,0:T(8,128)(2,1)S(1)} %copy-done), custom_call_target="tpu_custom_call" | custom-call | flops 50331648 | bytes 2097152 | tf_op jit(solution)/shard_map/pallas_call | solution.py:205
  48.3 3.2 %collective-permute-start.2 = (f32[24,2048]{1,0:T(8,128)S(1)}, f32[24,2048]{1,0:T(8,128)S(1)}, u32[]{:S(2)}, u32[]{:S(2)}) collective-permute-start(f32[24,2048]{1,0:T(8,128)S(1)} %get-tuple-element.12), channel_id=1, source_target_pairs={{0,1},{1,0},{2,3},{3,2},{4,5},{5,4},{6,7},{7,6},{8,9},{9,8},{10,11... | collective-permute-start | bytes 589832 | tf_op jit(solution)/shard_map/ppermute | solution.py:240
  51.5 0.5 shard_map.75
  52.0 0.0 collective-permute-start.1
  52.0 0.5 shard_map.76
  52.5 0.1 collective-permute-done.2
  52.6 2.2 %collective-permute-start.3 = (bf16[24,2048]{1,0:T(8,128)(2,1)S(1)}, bf16[24,2048]{1,0:T(8,128)(2,1)S(1)}, u32[]{:S(2)}, u32[]{:S(2)}) collective-permute-start(bf16[24,2048]{1,0:T(8,128)(2,1)S(1)} %add_convert_fusion.1), channel_id=1, source_target_pairs={{0,2},{1,3},{2,0},{3,1},{4,6},{5,7},{6,4},{7,5},{8,10},{9,11},{10,... | collective-permute-start | bytes 294920 | tf_op jit(solution)/shard_map/ppermute | solution.py:243
  54.8 0.5 shard_map.74
  55.2 0.0 collective-permute-done.1
  55.2 2.9 %collective-permute-done.3 = bf16[24,2048]{1,0:T(8,128)(2,1)S(1)} collective-permute-done((bf16[24,2048]{1,0:T(8,128)(2,1)S(1)}, bf16[24,2048]{1,0:T(8,128)(2,1)S(1)}, u32[]{:S(2)}, u32[]{:S(2)}) %collective-permute-start.3) | collective-permute-done | bytes 98336 | tf_op jit(solution)/shard_map/ppermute | solution.py:243
  58.1 0.7 %convert_add_fusion = f32[24,2048]{1,0:T(8,128)} fusion(bf16[24,2048]{1,0:T(8,128)(2,1)S(1)} %collective-permute-done.3, f32[24,2048]{1,0:T(8,128)S(1)} %shard_map.74, f32[24,2048]{1,0:T(8,128)S(1)} %collective-permute-done.1), kind=kLoop, calls=%fused_computation.1 | loop fusion | flops 147456 | bytes 688128 | tf_op jit(solution)/shard_map/add | solution.py:247
  (1 shorter events, 0.0 us)
Async XLA Ops:
  0.0 47.5 %copy-start = (bf16[2,256,8192]{2,1,0:T(8,128)(2,1)S(1)}, bf16[2,256,8192]{2,1,0:T(8,128)(2,1)}, u32[]{:S(2)}) copy-start(bf16[2,256,8192]{2,1,0:T(8,128)(2,1)} %basis_ref.7) | copy-start | bytes 25165828
  0.0 47.5 %copy-start.1 = (s32[4,24]{1,0:T(4,128)S(1)}, s32[4,24]{1,0:T(4,128)}, u32[]{:S(2)}) copy-start(s32[4,24]{1,0:T(4,128)} %index_ref.1) | copy-start | bytes 1156
  7.9 3.2 %collective-permute-start = (bf16[32,2,16,256]{3,2,1,0:T(8,128)(2,1)}, bf16[32,2,16,256]{3,2,1,0:T(8,128)(2,1)S(1)}, u32[]{:S(2)}, u32[]{:S(2)}) collective-permute-start(bf16[32,2,16,256]{3,2,1,0:T(8,128)(2,1)} %get-tuple-element.10), channel_id=1, source_target_pairs={{0,1},{1,0},{2,3},{3,2},{4,5},{5,4},{6,7},{7,6},{8,9},{9,8},{10,11... | collective-permute-start | bytes 1572872 | tf_op jit(solution)/shard_map/ppermute | solution.py:231
  48.3 4.3 %collective-permute-start.2 = (f32[24,2048]{1,0:T(8,128)S(1)}, f32[24,2048]{1,0:T(8,128)S(1)}, u32[]{:S(2)}, u32[]{:S(2)}) collective-permute-start(f32[24,2048]{1,0:T(8,128)S(1)} %get-tuple-element.12), channel_id=1, source_target_pairs={{0,1},{1,0},{2,3},{3,2},{4,5},{5,4},{6,7},{7,6},{8,9},{9,8},{10,11... | collective-permute-start | bytes 589832 | tf_op jit(solution)/shard_map/ppermute | solution.py:240
  52.0 3.3 %collective-permute-start.1 = (f32[24,2048]{1,0:T(8,128)S(1)}, f32[24,2048]{1,0:T(8,128)S(1)}, u32[]{:S(2)}, u32[]{:S(2)}) collective-permute-start(f32[24,2048]{1,0:T(8,128)S(1)} %shard_map.75), channel_id=1, source_target_pairs={{0,1},{1,0},{2,3},{3,2},{4,5},{5,4},{6,7},{7,6},{8,9},{9,8},{10,11... | collective-permute-start | bytes 589832 | tf_op jit(solution)/shard_map/ppermute | solution.py:245
  52.6 5.5 %collective-permute-start.3 = (bf16[24,2048]{1,0:T(8,128)(2,1)S(1)}, bf16[24,2048]{1,0:T(8,128)(2,1)S(1)}, u32[]{:S(2)}, u32[]{:S(2)}) collective-permute-start(bf16[24,2048]{1,0:T(8,128)(2,1)S(1)} %add_convert_fusion.1), channel_id=1, source_target_pairs={{0,2},{1,3},{2,0},{3,1},{4,6},{5,7},{6,4},{7,5},{8,10},{9,11},{10,... | collective-permute-start | bytes 294920 | tf_op jit(solution)/shard_map/ppermute | solution.py:243

commit v4 on v3

--- a/solution.py
+++ b/solution.py
@@ -42,59 +42,75 @@
 
 def stack_kernel(
     group, window_hbm, slot_hbm, table_hbm, ray_hbm, trace_hbm, mine_ref, other_ref,
-    buffer, window_ref, slot_ref, table_ref, ray_ref, weight_ref, acc_ref, sems, trace_sems,
+    buffer, window_ref, slot_ref, table_ref, ray_ref, weight_ref, factor_ref, high_ref, low_ref,
+    acc_ref, sems, trace_sems,
 ):
     rays, doubled = ray_ref.shape
     half = doubled // 2
     shots, per_shot, _ = trace_hbm.shape
-    pairs = ((window_hbm, window_ref), (ray_hbm, ray_ref), (slot_hbm, slot_ref), (table_hbm, table_ref))
+    groups = shots // group
+    pairs = ((slot_hbm, slot_ref), (table_hbm, table_ref), (ray_hbm, ray_ref), (window_hbm, window_ref))
     small = [pltpu.make_async_copy(a, b, sems.at[i]) for i, (a, b) in enumerate(pairs)]
     loads = []
-    for g in range(shots // group):
+    for g in range(groups):
         part = pl.ds(g * group, group)
         loads.append(pltpu.make_async_copy(trace_hbm.at[part], buffer.at[part], trace_sems.at[g]))
     for copy in small + loads:
         copy.start()
     _, core = beam_position()
     acc_ref[...] = jnp.zeros_like(acc_ref)
+
+    small[0].wait()
     small[1].wait()
+    slot_rows = lax.broadcasted_iota(jnp.int32, (128, per_shot), 0)
+    for first in range(0, shots, 2):
+        picks = []
+        for shot in (first, first + 1):
+            slots = slot_ref[shot : shot + 1, :]
+            picks.append((slot_rows == slots).astype(F32).astype(BF16))
+        both = jnp.dot(
+            table_ref[...], jnp.concatenate(picks, axis=1), preferred_element_type=F32
+        ).astype(BF16)
+        for i in range(2):
+            left = both[:, i * per_shot : (i + 1) * per_shot]
+            factor_ref[first + i, :, :per_shot] = left
+            factor_ref[first + i, :, per_shot:] = jnp.concatenate(
+                [left[64:128], -left[:64], left[192:], -left[128:192]], axis=0
+            )
+    small[2].wait()
     weight_ref[:rays, :half] = ray_ref[:, :half]
     weight_ref[:rays, half:] = -ray_ref[:, half:]
     weight_ref[rays:, :half] = ray_ref[:, half:]
     weight_ref[rays:, half:] = ray_ref[:, :half]
-    for copy in (small[0], small[2], small[3]):
-        copy.wait()
-    slot_rows = lax.broadcasted_iota(jnp.int32, (128, per_shot), 0)
-    for g in range(shots // group):
-        first = g * group
-        factors = []
-        for j in range(0, group, 2):
-            picks = []
-            for shot in (first + j, first + j + 1):
-                slots = slot_ref[shot : shot + 1, :]
-                picks.append((slot_rows == slots).astype(F32).astype(BF16))
-            both = jnp.dot(
-                table_ref[...], jnp.concatenate(picks, axis=1), preferred_element_type=F32
-            ).astype(BF16)
-            for i in range(2):
-                left = both[:, i * per_shot : (i + 1) * per_shot]
-                right = jnp.concatenate(
-                    [left[64:128], -left[:64], left[192:], -left[128:192]], axis=0
-                )
-                factors.append(jnp.concatenate([left, right], axis=1))
-        loads[g].wait()
-        samples = buffer[first : first + group].reshape(group * per_shot, doubled)
-        value = lax.dot_general(samples, weight_ref[...], NT, preferred_element_type=F32)
-        high, low = split(value)
+    small[3].wait()
+
+    def slant(g):
+        slot = g % 2
         for j in range(group):
+            shot = g * group + j
             rows = slice(j * per_shot, (j + 1) * per_shot)
-            right_high = jnp.concatenate([high[rows, :rays], high[rows, rays:]], axis=0)
-            right_low = jnp.concatenate([low[rows, :rays], low[rows, rays:]], axis=0)
-            one = jnp.dot(factors[j], right_high, preferred_element_type=F32)
-            two = jnp.dot(factors[j][:128], right_low, preferred_element_type=F32)
-            window = window_ref[first + j]
+            right_high = jnp.concatenate(
+                [high_ref[slot, rows, :rays], high_ref[slot, rows, rays:]], axis=0
+            )
+            right_low = jnp.concatenate(
+                [low_ref[slot, rows, :rays], low_ref[slot, rows, rays:]], axis=0
+            )
+            one = jnp.dot(factor_ref[shot], right_high, preferred_element_type=F32)
+            two = jnp.dot(factor_ref[shot, :128], right_low, preferred_element_type=F32)
+            window = window_ref[shot]
             away = ((window >> 2) & 1) ^ core
             acc_ref[away * 8 + (window >> 3) * 4 + (window & 3)] += one[:128] + one[128:] + two
+
+    for g in range(groups):
+        if g < 2:
+            for load in loads[g : 1 if g == 0 else groups]:
+                load.wait()
+        samples = buffer[g * group : (g + 1) * group].reshape(group * per_shot, doubled)
+        value = lax.dot_general(samples, weight_ref[...], NT, preferred_element_type=F32)
+        high_ref[g % 2], low_ref[g % 2] = split(value)
+        if g > 0:
+            slant(g - 1)
+    slant(groups - 1)
     for side in range(2):
         for wl in range(WIN_OWN):
             for h in range(2):
@@ -106,10 +122,12 @@
                 other_ref[at : at + 4, side] = block.reshape(4, 16, rays)
 
 
-def stack(window, slots, table, ray_phase, traces):
-    shots, _, doubled = traces.shape
+def stack(*operands):
+    window, slots, table, ray_phase, traces = operands
+    shots, per_shot, doubled = traces.shape
     rays = ray_phase.shape[0]
     group = 4
+    value = pltpu.VMEM((2, group * per_shot, 2 * rays), BF16)
     return pl.pallas_call(
         functools.partial(stack_kernel, group),
         out_shape=(
@@ -125,16 +143,19 @@
             pltpu.VMEM(table.shape, BF16),
             pltpu.VMEM(ray_phase.shape, BF16),
             pltpu.VMEM((2 * rays, doubled), BF16),
+            pltpu.VMEM((shots, 256, 2 * per_shot), BF16),
+            value,
+            value,
             pltpu.VMEM((16, 2 * P_SIZE, rays), F32),
             pltpu.SemaphoreType.DMA((4,)),
             pltpu.SemaphoreType.DMA((shots // group,)),
         ],
         compiler_params=pltpu.CompilerParams(vmem_limit_bytes=STACK_VMEM),
         name="stack",
-    )(window, slots, table, ray_phase, traces)
-
-
-STACK_VMEM = 54 << 20
+    )(*[pltpu.with_memory_space_constraint(jnp.asarray(x), pltpu.HBM) for x in operands])
+
+
+STACK_VMEM = 48 << 20
 IMAGE_VMEM = 12 << 20
 
 

time: 59.1 us -> 55.3 us (0.936)
  Pallas kernels: 10.1 us -> 7.86 us
  other arithmetic: 2.12 us -> 0.9 us
    pallas_call x1, Pallas kernels: 7.91 us -> 5.66 us  [stack(): pl.pallas_call(functools.partial(stack_kernel, group), out_shape=(jax.Sha...]
    convert_element_type x1, other arithmetic: 1.39 us -> 0.18 us  [body(): both = (mine + other.astype(F32)).astype(BF16).reshape(2 * slabs, 16, rays)]
where the time goes in v4:
time: 55.3 us; the launch traced here: 55.2 us
  blocking collectives  34.9 us (63%)
  Pallas kernels  7.86 us (14%)
  starting transfers between devices  6.91 us (12%)
  waiting for transfers between devices  4.58 us (8%)
  other arithmetic  0.9 us (2%)
    all_to_all x1, blocking collectives, body(): lax.all_to_all(both, AXES, 0, 0, axis_index_groups=same_core, tiled=True)  23.6 us
    all_to_all x1, blocking collectives, body(): table = lax.all_to_all(spread(arrived), 'slab', 0, 0, tiled=True)  11.3 us
    pallas_call x1, Pallas kernels, stack(): pl.pallas_call(functools.partial(stack_kernel, group), out_shape=(jax.Sha...  5.66 us
    ppermute x1, starting transfers between devices, body(): far_other = lax.ppermute(far_other, AXES, partner)  3.25 us
    ppermute x1, waiting for transfers between devices, body(): far = lax.ppermute(far, AXES, distant)  2.93 us
    ppermute x1, starting transfers between devices, body(): far = lax.ppermute(far, AXES, distant)  2.16 us
    pallas_call x4, Pallas kernels, image_call(): pl.pallas_call(kernel, out_shape=(shape, wave) if wave_out else shape, in...  2.1 us
    ppermute x1, waiting for transfers between devices, body(): other = lax.ppermute(other, AXES, partner)  1.54 us
  transfers between devices with their start and end apart: 4, of which 3 were waited for; matrix products, arithmetic and copies ran while one was open for 0% of the time, Pallas kernels for 2%

profile of v4, /device:TPU:1, one launch (start us, length us, event | category | flops | bytes accessed | tf_op | source)
XLA Modules:
  0.0 55.2 jit_solution(7998239120884795995)
XLA Ops:
  0.0 0.0 copy-start
  0.0 0.0 copy-start.1
  0.0 5.7 %stack.1 = (f32[32,2,16,256]{3,2,1,0:T(8,128)S(1)}, bf16[32,2,16,256]{3,2,1,0:T(8,128)(2,1)S(1)}) custom-call(s32[16]{0:T(128)} %window_hbm.1, s32[16,128]{1,0:T(8,128)} %slot_hbm.1, bf16[256,128]{1,0:T(8,128)(2,1)} %constant.2.clone.table_hbm, bf16[256,1024]{1,0:T(8,128)(2,1)} %ray_hbm.1, bf16[16,128,1024]{2,1,0:T(8,128)(2,1)} %trace_hbm.1), custom_call_target="tpu_custom_call" | custom-call | tf_op jit(solution)/shard_map/stack/pallas_call | solution.py:131
  5.7 1.5 %collective-permute-start = (bf16[32,2,16,256]{3,2,1,0:T(8,128)(2,1)S(1)}, bf16[32,2,16,256]{3,2,1,0:T(8,128)(2,1)S(1)}, u32[]{:S(2)}, u32[]{:S(2)}) collective-permute-start(bf16[32,2,16,256]{3,2,1,0:T(8,128)(2,1)S(1)} %get-tuple-element.10), channel_id=1, source_target_pairs={{0,1},{1,0},{2,3},{3,2},{4,5},{5,4},{6,7},{7,6},{8,9},{9,8},{10,11... | collective-permute-start | bytes 1572872 | tf_op jit(solution)/shard_map/ppermute | solution.py:252
  7.1 1.5 %collective-permute-done = bf16[32,2,16,256]{3,2,1,0:T(8,128)(2,1)S(1)} collective-permute-done((bf16[32,2,16,256]{3,2,1,0:T(8,128)(2,1)S(1)}, bf16[32,2,16,256]{3,2,1,0:T(8,128)(2,1)S(1)}, u32[]{:S(2)}, u32[]{:S(2)}) %collective-permute-start) | collective-permute-done | bytes 524320 | tf_op jit(solution)/shard_map/ppermute | solution.py:252
  8.7 0.2 add_convert_fusion
  8.9 23.6 %all_to_all.10.arrived_ref = bf16[64,16,256]{2,1,0:T(8,128)(2,1)S(1)} all-to-all(bf16[64,16,256]{2,1,0:T(8,128)(2,1)S(1)} %bitcast.1), channel_id=1, replica_groups={{0,2,4,6,8,10,12,14,16,18,20,22,24,26,28,30,32,34,36,38,40,42,44,46,48,..., dimensions={0} | all-to-all | bytes 1048576 | tf_op jit(solution)/shard_map/all_to_all | solution.py:254
  32.5 0.1 spread.1
  32.6 11.3 %all_to_all.11.table_ref = bf16[32,16,256]{2,1,0:T(8,128)(2,1)S(1)} all-to-all(bf16[32,16,256]{2,1,0:T(8,128)(2,1)S(1)} %spread.1), channel_id=1, replica_groups=mesh['slab'=32,'beam'=4] {'slab'}, dimensions={0} | all-to-all | bytes 524288 | tf_op jit(solution)/shard_map/all_to_all | solution.py:255
  43.8 0.0 copy-done
  43.8 0.0 copy-done.1
  43.8 0.7 %shard_map.73 = (f32[24,2048]{1,0:T(8,128)S(1)}, bf16[24,512]{1,0:T(8,128)(2,1)S(1)}) custom-call(s32[4,24]{1,0:T(4,128)S(1)} %copy-done.1, bf16[32,16,256]{2,1,0:T(8,128)(2,1)S(1)} %all_to_all.11.table_ref, bf16[2,256,8192]{2,1,0:T(8,128)(2,1)S(1)} %copy-done), custom_call_target="tpu_custom_call" | custom-call | flops 50331648 | bytes 2097152 | tf_op jit(solution)/shard_map/pallas_call | solution.py:226
  44.6 3.2 %collective-permute-start.2 = (f32[24,2048]{1,0:T(8,128)S(1)}, f32[24,2048]{1,0:T(8,128)S(1)}, u32[]{:S(2)}, u32[]{:S(2)}) collective-permute-start(f32[24,2048]{1,0:T(8,128)S(1)} %get-tuple-element.12), channel_id=1, source_target_pairs={{0,1},{1,0},{2,3},{3,2},{4,5},{5,4},{6,7},{7,6},{8,9},{9,8},{10,11... | collective-permute-start | bytes 589832 | tf_op jit(solution)/shard_map/ppermute | solution.py:261
  47.8 0.5 shard_map.75
  48.3 0.0 collective-permute-start.1
  48.3 0.5 shard_map.76
  48.8 0.1 collective-permute-done.2
  48.9 2.2 %collective-permute-start.3 = (bf16[24,2048]{1,0:T(8,128)(2,1)S(1)}, bf16[24,2048]{1,0:T(8,128)(2,1)S(1)}, u32[]{:S(2)}, u32[]{:S(2)}) collective-permute-start(bf16[24,2048]{1,0:T(8,128)(2,1)S(1)} %add_convert_fusion.1), channel_id=1, source_target_pairs={{0,2},{1,3},{2,0},{3,1},{4,6},{5,7},{6,4},{7,5},{8,10},{9,11},{10,... | collective-permute-start | bytes 294920 | tf_op jit(solution)/shard_map/ppermute | solution.py:264
  51.1 0.5 shard_map.74
  51.5 0.0 collective-permute-done.1
  51.5 2.9 %collective-permute-done.3 = bf16[24,2048]{1,0:T(8,128)(2,1)S(1)} collective-permute-done((bf16[24,2048]{1,0:T(8,128)(2,1)S(1)}, bf16[24,2048]{1,0:T(8,128)(2,1)S(1)}, u32[]{:S(2)}, u32[]{:S(2)}) %collective-permute-start.3) | collective-permute-done | bytes 98336 | tf_op jit(solution)/shard_map/ppermute | solution.py:264
  54.5 0.7 %convert_add_fusion = f32[24,2048]{1,0:T(8,128)} fusion(bf16[24,2048]{1,0:T(8,128)(2,1)S(1)} %collective-permute-done.3, f32[24,2048]{1,0:T(8,128)S(1)} %shard_map.74, f32[24,2048]{1,0:T(8,128)S(1)} %collective-permute-done.1), kind=kLoop, calls=%fused_computation.1 | loop fusion | flops 147456 | bytes 688128 | tf_op jit(solution)/shard_map/add | solution.py:268
  (1 shorter events, 0.0 us)
Async XLA Ops:
  0.0 43.8 %copy-start = (bf16[2,256,8192]{2,1,0:T(8,128)(2,1)S(1)}, bf16[2,256,8192]{2,1,0:T(8,128)(2,1)}, u32[]{:S(2)}) copy-start(bf16[2,256,8192]{2,1,0:T(8,128)(2,1)} %basis_ref.7) | copy-start | bytes 25165828
  0.0 43.8 %copy-start.1 = (s32[4,24]{1,0:T(4,128)S(1)}, s32[4,24]{1,0:T(4,128)}, u32[]{:S(2)}) copy-start(s32[4,24]{1,0:T(4,128)} %index_ref.1) | copy-start | bytes 1156
  5.7 3.0 %collective-permute-start = (bf16[32,2,16,256]{3,2,1,0:T(8,128)(2,1)S(1)}, bf16[32,2,16,256]{3,2,1,0:T(8,128)(2,1)S(1)}, u32[]{:S(2)}, u32[]{:S(2)}) collective-permute-start(bf16[32,2,16,256]{3,2,1,0:T(8,128)(2,1)S(1)} %get-tuple-element.10), channel_id=1, source_target_pairs={{0,1},{1,0},{2,3},{3,2},{4,5},{5,4},{6,7},{7,6},{8,9},{9,8},{10,11... | collective-permute-start | bytes 1572872 | tf_op jit(solution)/shard_map/ppermute | solution.py:252
  44.6 4.3 %collective-permute-start.2 = (f32[24,2048]{1,0:T(8,128)S(1)}, f32[24,2048]{1,0:T(8,128)S(1)}, u32[]{:S(2)}, u32[]{:S(2)}) collective-permute-start(f32[24,2048]{1,0:T(8,128)S(1)} %get-tuple-element.12), channel_id=1, source_target_pairs={{0,1},{1,0},{2,3},{3,2},{4,5},{5,4},{6,7},{7,6},{8,9},{9,8},{10,11... | collective-permute-start | bytes 589832 | tf_op jit(solution)/shard_map/ppermute | solution.py:261
  48.3 3.3 %collective-permute-start.1 = (f32[24,2048]{1,0:T(8,128)S(1)}, f32[24,2048]{1,0:T(8,128)S(1)}, u32[]{:S(2)}, u32[]{:S(2)}) collective-permute-start(f32[24,2048]{1,0:T(8,128)S(1)} %shard_map.75), channel_id=1, source_target_pairs={{0,1},{1,0},{2,3},{3,2},{4,5},{5,4},{6,7},{7,6},{8,9},{9,8},{10,11... | collective-permute-start | bytes 589832 | tf_op jit(solution)/shard_map/ppermute | solution.py:266
  48.9 5.5 %collective-permute-start.3 = (bf16[24,2048]{1,0:T(8,128)(2,1)S(1)}, bf16[24,2048]{1,0:T(8,128)(2,1)S(1)}, u32[]{:S(2)}, u32[]{:S(2)}) collective-permute-start(bf16[24,2048]{1,0:T(8,128)(2,1)S(1)} %add_convert_fusion.1), channel_id=1, source_target_pairs={{0,2},{1,3},{2,0},{3,1},{4,6},{5,7},{6,4},{7,5},{8,10},{9,11},{10,... | collective-permute-start | bytes 294920 | tf_op jit(solution)/shard_map/ppermute | solution.py:264

commit v5 on v3

--- a/solution.py
+++ b/solution.py
@@ -40,101 +40,182 @@
     return lax.div(position, 2), lax.rem(position, 2)
 
 
-def stack_kernel(
-    group, window_hbm, slot_hbm, table_hbm, ray_hbm, trace_hbm, mine_ref, other_ref,
-    buffer, window_ref, slot_ref, table_ref, ray_ref, weight_ref, acc_ref, sems, trace_sems,
+def order_shots(window_ref, order_ref, core):
+    shots = order_ref.shape[0]
+    others = jnp.int32(0)
+    for shot in range(shots):
+        away = ((window_ref[shot] >> 2) & 1) ^ core
+        order_ref[jnp.where(away == 1, others, shots // 2 + shot - others)] = shot
+        others = others + away
+
+
+def accumulate(groups, base, window_ref, order_ref, buffer, weight_ref, factor_ref, high_ref, low_ref, acc_ref, wait):
+    per_shot, doubled = buffer.shape[1:]
+    rays = weight_ref.shape[0] // 2
+
+    def slant(slot, rows):
+        high = jnp.concatenate([high_ref[rows, :rays], high_ref[rows, rays:]], axis=0)
+        low = jnp.concatenate([low_ref[rows, :rays], low_ref[rows, rays:]], axis=0)
+        one = jnp.dot(factor_ref[slot], high, preferred_element_type=F32)
+        two = jnp.dot(factor_ref[slot, :128], low, preferred_element_type=F32)
+        window = window_ref[order_ref[base + slot]]
+        acc_ref[(window >> 3) * WIN_OWN + (window & 3)] += one[:128] + one[128:] + two
+
+    pending, first = [], 0
+    for group in groups:
+        wait(first, group)
+        samples = buffer[base + first : base + first + group].reshape(group * per_shot, doubled)
+        value = lax.dot_general(samples, weight_ref[...], NT, preferred_element_type=F32)
+        all_rows = slice(first * per_shot, (first + group) * per_shot)
+        high_ref[all_rows], low_ref[all_rows] = split(value)
+        for slot in pending:
+            slant(slot, slice(slot * per_shot, (slot + 1) * per_shot))
+        pending = range(first, first + group)
+        first += group
+    for slot in pending:
+        slant(slot, slice(slot * per_shot, (slot + 1) * per_shot))
+
+
+def put_sums(acc_ref, out_ref):
+    rays = out_ref.shape[-1]
+    for side in range(2):
+        for wl in range(WIN_OWN):
+            for h in range(2):
+                at = h * 16 + wl * 4
+                block = acc_ref[side * 4 + wl, h * 64 : (h + 1) * 64]
+                out_ref[at : at + 4, side] = block.astype(out_ref.dtype).reshape(4, 16, rays)
+
+
+def other_kernel(
+    window_hbm, slot_hbm, table_hbm, ray_hbm, trace_hbm, out_ref, buffer, weight_ref, mine_ref,
+    window_ref, order_ref, slot_ref, table_ref, ray_ref, factor_ref, high_ref, low_ref, acc_ref,
+    sems, trace_sems,
 ):
     rays, doubled = ray_ref.shape
     half = doubled // 2
     shots, per_shot, _ = trace_hbm.shape
-    pairs = ((window_hbm, window_ref), (ray_hbm, ray_ref), (slot_hbm, slot_ref), (table_hbm, table_ref))
+    _, core = beam_position()
+    pairs = ((window_hbm, window_ref), (slot_hbm, slot_ref), (table_hbm, table_ref), (ray_hbm, ray_ref))
     small = [pltpu.make_async_copy(a, b, sems.at[i]) for i, (a, b) in enumerate(pairs)]
-    loads = []
-    for g in range(shots // group):
-        part = pl.ds(g * group, group)
-        loads.append(pltpu.make_async_copy(trace_hbm.at[part], buffer.at[part], trace_sems.at[g]))
-    for copy in small + loads:
+    for copy in small:
         copy.start()
-    _, core = beam_position()
     acc_ref[...] = jnp.zeros_like(acc_ref)
+    small[0].wait()
+    order_shots(window_ref, order_ref, core)
+    load = lambda shot, slot: pltpu.make_async_copy(
+        trace_hbm.at[shot], buffer.at[slot], trace_sems.at[slot]
+    )
+    for slot in range(shots):
+        load(order_ref[slot], slot).start()
+
     small[1].wait()
-    weight_ref[:rays, :half] = ray_ref[:, :half]
-    weight_ref[:rays, half:] = -ray_ref[:, half:]
-    weight_ref[rays:, :half] = ray_ref[:, half:]
-    weight_ref[rays:, half:] = ray_ref[:, :half]
-    for copy in (small[0], small[2], small[3]):
-        copy.wait()
+    small[2].wait()
     slot_rows = lax.broadcasted_iota(jnp.int32, (128, per_shot), 0)
-    for g in range(shots // group):
-        first = g * group
-        factors = []
-        for j in range(0, group, 2):
+
+    def build(target, base):
+        for first in range(0, shots // 2, 2):
             picks = []
-            for shot in (first + j, first + j + 1):
-                slots = slot_ref[shot : shot + 1, :]
+            for slot in (base + first, base + first + 1):
+                slots = slot_ref[pl.ds(order_ref[slot], 1), :]
                 picks.append((slot_rows == slots).astype(F32).astype(BF16))
             both = jnp.dot(
                 table_ref[...], jnp.concatenate(picks, axis=1), preferred_element_type=F32
             ).astype(BF16)
             for i in range(2):
                 left = both[:, i * per_shot : (i + 1) * per_shot]
-                right = jnp.concatenate(
+                target[first + i, :, :per_shot] = left
+                target[first + i, :, per_shot:] = jnp.concatenate(
                     [left[64:128], -left[:64], left[192:], -left[128:192]], axis=0
                 )
-                factors.append(jnp.concatenate([left, right], axis=1))
-        loads[g].wait()
-        samples = buffer[first : first + group].reshape(group * per_shot, doubled)
-        value = lax.dot_general(samples, weight_ref[...], NT, preferred_element_type=F32)
-        high, low = split(value)
-        for j in range(group):
-            rows = slice(j * per_shot, (j + 1) * per_shot)
-            right_high = jnp.concatenate([high[rows, :rays], high[rows, rays:]], axis=0)
-            right_low = jnp.concatenate([low[rows, :rays], low[rows, rays:]], axis=0)
-            one = jnp.dot(factors[j], right_high, preferred_element_type=F32)
-            two = jnp.dot(factors[j][:128], right_low, preferred_element_type=F32)
-            window = window_ref[first + j]
-            away = ((window >> 2) & 1) ^ core
-            acc_ref[away * 8 + (window >> 3) * 4 + (window & 3)] += one[:128] + one[128:] + two
-    for side in range(2):
-        for wl in range(WIN_OWN):
-            for h in range(2):
-                at = h * 16 + wl * 4
-                rows = slice(h * 64, (h + 1) * 64)
-                block = acc_ref[side * 4 + wl, rows]
-                mine_ref[at : at + 4, side] = block.reshape(4, 16, rays)
-                block = acc_ref[8 + side * 4 + wl, rows].astype(other_ref.dtype)
-                other_ref[at : at + 4, side] = block.reshape(4, 16, rays)
-
-
-def stack(window, slots, table, ray_phase, traces):
-    shots, _, doubled = traces.shape
+
+    build(factor_ref, 0)
+    build(mine_ref, shots // 2)
+    small[3].wait()
+    weight_ref[:rays, :half] = ray_ref[:, :half]
+    weight_ref[:rays, half:] = -ray_ref[:, half:]
+    weight_ref[rays:, :half] = ray_ref[:, half:]
+    weight_ref[rays:, half:] = ray_ref[:, :half]
+
+    def wait(first, count):
+        for slot in range(first, first + count):
+            load(0, slot).wait()
+
+    accumulate(
+        (4, 4), 0, window_ref, order_ref, buffer, weight_ref, factor_ref, high_ref, low_ref,
+        acc_ref, wait,
+    )
+    put_sums(acc_ref, out_ref)
+    wait(shots // 2, shots // 2)
+
+
+def mine_kernel(
+    window_hbm, buffer, weight_ref, factor_ref, out_ref, window_ref, order_ref, high_ref,
+    low_ref, acc_ref, sem,
+):
+    copy = pltpu.make_async_copy(window_hbm, window_ref, sem)
+    copy.start()
+    acc_ref[...] = jnp.zeros_like(acc_ref)
+    _, core = beam_position()
+    copy.wait()
+    order_shots(window_ref, order_ref, core)
+    accumulate(
+        (8,), 8, window_ref, order_ref, buffer, weight_ref, factor_ref, high_ref, low_ref,
+        acc_ref, lambda first, count: None,
+    )
+    put_sums(acc_ref, out_ref)
+
+
+def stack(*operands):
+    operands = [pltpu.with_memory_space_constraint(jnp.asarray(x), pltpu.HBM) for x in operands]
+    window, slots, table, ray_phase, traces = operands
+    shots, per_shot, doubled = traces.shape
     rays = ray_phase.shape[0]
-    group = 4
-    return pl.pallas_call(
-        functools.partial(stack_kernel, group),
+    value = pltpu.VMEM((shots // 2 * per_shot, 2 * rays), BF16)
+    scalars = pltpu.SMEM(window.shape, jnp.int32)
+    acc = pltpu.VMEM((8, 2 * P_SIZE, rays), F32)
+    shape = jax.ShapeDtypeStruct
+    factor = shape((shots // 2, 256, 2 * per_shot), BF16)
+    other, buffer, weight, factor = pl.pallas_call(
+        other_kernel,
         out_shape=(
-            jax.ShapeDtypeStruct((32, 2, 16, rays), F32),
-            jax.ShapeDtypeStruct((32, 2, 16, rays), BF16),
+            shape((32, 2, 16, rays), BF16),
+            shape(traces.shape, BF16),
+            shape((2 * rays, doubled), BF16),
+            factor,
         ),
         in_specs=[HBM] * 5,
-        out_specs=(VMEM, VMEM),
+        out_specs=(VMEM,) * 4,
         scratch_shapes=[
-            pltpu.VMEM(traces.shape, BF16),
-            pltpu.SMEM(window.shape, jnp.int32),
+            scalars,
+            scalars,
             pltpu.VMEM(slots.shape, jnp.int32),
             pltpu.VMEM(table.shape, BF16),
             pltpu.VMEM(ray_phase.shape, BF16),
-            pltpu.VMEM((2 * rays, doubled), BF16),
-            pltpu.VMEM((16, 2 * P_SIZE, rays), F32),
+            pltpu.VMEM(factor.shape, BF16),
+            value,
+            value,
+            acc,
             pltpu.SemaphoreType.DMA((4,)),
-            pltpu.SemaphoreType.DMA((shots // group,)),
+            pltpu.SemaphoreType.DMA((shots,)),
         ],
         compiler_params=pltpu.CompilerParams(vmem_limit_bytes=STACK_VMEM),
-        name="stack",
-    )(window, slots, table, ray_phase, traces)
-
-
-STACK_VMEM = 54 << 20
+        name="stack_other",
+    )(*operands)
+    mine = lambda: pl.pallas_call(
+        mine_kernel,
+        out_shape=shape((32, 2, 16, rays), F32),
+        in_specs=[HBM, VMEM, VMEM, VMEM],
+        out_specs=VMEM,
+        scratch_shapes=[scalars, scalars, value, value, acc, pltpu.SemaphoreType.DMA],
+        compiler_params=pltpu.CompilerParams(vmem_limit_bytes=MINE_VMEM),
+        cost_estimate=pl.CostEstimate(flops=2 << 30, bytes_accessed=8 << 20, transcendentals=0),
+        name="stack_mine",
+    )(window, buffer, weight, factor)
+    return other, mine
+
+
+STACK_VMEM = 32 << 20
+MINE_VMEM = 24 << 20
 IMAGE_VMEM = 12 << 20
 
 
@@ -227,9 +308,9 @@
     distant = [(i, i ^ 2) for i in range(devices)]
     same_core = [list(range(core, devices, 2)) for core in range(2)]
 
-    mine, other = stack(shot_window, trace_slot, slant_table(scale), ray_phase, traces)
+    other, mine = stack(shot_window, trace_slot, slant_table(scale), ray_phase, traces)
     other = lax.ppermute(other, AXES, partner)
-    both = (mine + other.astype(F32)).astype(BF16).reshape(2 * slabs, 16, rays)
+    both = (mine() + other.astype(F32)).astype(BF16).reshape(2 * slabs, 16, rays)
     arrived = lax.all_to_all(both, AXES, 0, 0, axis_index_groups=same_core, tiled=True)
     table = lax.all_to_all(spread(arrived), "slab", 0, 0, tiled=True)
 

time: 59.1 us -> 55.1 us (0.932)
  waiting for transfers between devices: 4.79 us -> 3.05 us
  other arithmetic: 2.12 us -> 0.9 us
  Pallas kernels: 10.1 us -> 9.15 us
    ppermute x1, waiting for transfers between devices: 1.75 us -> 0.01 us  [body(): other = lax.ppermute(other, AXES, partner)]
    convert_element_type x1, other arithmetic: 1.39 us -> 0.18 us  [body(): (mine() + other.astype(F32)).astype(BF16).reshape(2 * slabs, 16, rays)]
    pallas_call x1 -> x2, Pallas kernels: 7.91 us -> 6.96 us  [the longest x1 4.37 us: stack(): pl.pallas_call(other_kernel, out_shape=(shape((32, 2, 16, rays), BF16), s...]
  transfers between devices with their start and end apart: 4 -> 4, of which waited for: 3 -> 2; matrix products, arithmetic and copies ran while one was open for 0% -> 0% of each run, Pallas kernels for 2% -> 7%
where the time goes in v5:
time: 55.1 us; the launch traced here: 55 us
  blocking collectives  35.3 us (64%)
  Pallas kernels  9.15 us (17%)
  starting transfers between devices  6.53 us (12%)
  waiting for transfers between devices  3.05 us (6%)
  other arithmetic  0.9 us (2%)
    all_to_all x1, blocking collectives, body(): lax.all_to_all(both, AXES, 0, 0, axis_index_groups=same_core, tiled=True)  24 us
    all_to_all x1, blocking collectives, body(): table = lax.all_to_all(spread(arrived), 'slab', 0, 0, tiled=True)  11.3 us
    pallas_call x1, Pallas kernels, stack(): pl.pallas_call(other_kernel, out_shape=(shape((32, 2, 16, rays), BF16), s...  4.37 us
    ppermute x1, waiting for transfers between devices, body(): far = lax.ppermute(far, AXES, distant)  2.93 us
    ppermute x1, starting transfers between devices, body(): far_other = lax.ppermute(far_other, AXES, partner)  2.87 us
    pallas_call x1, Pallas kernels, stack(): pl.pallas_call(mine_kernel, out_shape=shape((32, 2, 16, rays), F32), in_s...  2.59 us
    ppermute x1, starting transfers between devices, body(): far = lax.ppermute(far, AXES, distant)  2.16 us
    pallas_call x4, Pallas kernels, image_call(): pl.pallas_call(kernel, out_shape=(shape, wave) if wave_out else shape, in...  2.1 us
  transfers between devices with their start and end apart: 4, of which 2 were waited for; matrix products, arithmetic and copies ran while one was open for 0% of the time, Pallas kernels for 7%

profile of v5, /device:TPU:1, one launch (start us, length us, event | category | flops | bytes accessed | tf_op | source)
XLA Modules:
  0.0 55.0 jit_solution(3701178988890949830)
XLA Ops:
  0.0 0.0 slice-start
  0.0 4.4 %stack_other.1 = (bf16[32,2,16,256]{3,2,1,0:T(8,128)(2,1)S(1)}, bf16[16,128,1024]{2,1,0:T(8,128)(2,1)S(1)}, bf16[512,1024]{1,0:T(8,128)(2,1)S(1)}, bf16[8,256,256]{2,1,0:T(8,128)(2,1)S(1)}) custom-call(s32[16]{0:T(128)} %window_hbm.3, s32[16,128]{1,0:T(8,128)} %slot_hbm.1, bf16[256,128]{1,0:T(8,128)(2,1)} %constant.2.clone.table_hbm, ...), custom_call_target="tpu_custom_call" | custom-call | tf_op jit(solution)/shard_map/stack_other/pallas_call | solution.py:178
  4.4 1.5 %collective-permute-start = (bf16[32,2,16,256]{3,2,1,0:T(8,128)(2,1)S(1)}, bf16[32,2,16,256]{3,2,1,0:T(8,128)(2,1)S(1)}, u32[]{:S(2)}, u32[]{:S(2)}) collective-permute-start(bf16[32,2,16,256]{3,2,1,0:T(8,128)(2,1)S(1)} %get-tuple-element.14), channel_id=1, source_target_pairs={{0,1},{1,0},{2,3},{3,2},{4,5},{5,4},{6,7},{7,6},{8,9},{9,8},{10,11... | collective-permute-start | bytes 1572872 | tf_op jit(solution)/shard_map/ppermute | solution.py:312
  5.8 0.0 slice-start.1
  5.8 2.6 %stack_mine.1 = f32[32,2,16,256]{3,2,1,0:T(8,128)S(1)} custom-call(s32[16]{0:T(128)} %window_hbm.3, bf16[16,128,1024]{2,1,0:T(8,128)(2,1)S(1)} %get-tuple-element.11.buffer, bf16[512,1024]{1,0:T(8,128)(2,1)S(1)} %get-tuple-element.12.weight_ref, bf16[8,256,256]{2,1,0:T(8,128)(2,1)S(1)} %get-tuple-element.13.factor_ref), custom_call_target="tpu_custom_call" | custom-call | flops 2147483648 | bytes 8388608 | tf_op jit(solution)/shard_map/stack_mine/pallas_call | solution.py:204
  8.4 0.0 copy-start
  8.5 0.0 collective-permute-done
  8.5 0.2 add_convert_fusion
  8.6 24.0 %all_to_all.10.arrived_ref = bf16[64,16,256]{2,1,0:T(8,128)(2,1)S(1)} all-to-all(bf16[64,16,256]{2,1,0:T(8,128)(2,1)S(1)} %bitcast.3), channel_id=1, replica_groups={{0,2,4,6,8,10,12,14,16,18,20,22,24,26,28,30,32,34,36,38,40,42,44,46,48,..., dimensions={0} | all-to-all | bytes 1048576 | tf_op jit(solution)/shard_map/all_to_all | solution.py:314
  32.6 0.1 spread.1
  32.7 11.3 %all_to_all.11.table_ref = bf16[32,16,256]{2,1,0:T(8,128)(2,1)S(1)} all-to-all(bf16[32,16,256]{2,1,0:T(8,128)(2,1)S(1)} %spread.1), channel_id=1, replica_groups=mesh['slab'=32,'beam'=4] {'slab'}, dimensions={0} | all-to-all | bytes 524288 | tf_op jit(solution)/shard_map/all_to_all | solution.py:315
  44.0 0.0 slice-done
  44.0 0.0 slice-done.1
  44.0 0.0 copy-done
  44.0 0.7 %shard_map.73 = (f32[24,2048]{1,0:T(8,128)S(1)}, bf16[24,512]{1,0:T(8,128)(2,1)S(1)}) custom-call(s32[4,24]{1,0:T(4,128)S(1)} %copy-done, bf16[32,16,256]{2,1,0:T(8,128)(2,1)S(1)} %all_to_all.11.table_ref, bf16[2,256,8192]{2,1,0:T(8,128)(2,1)S(1)} %bitcast.2), custom_call_target="tpu_custom_call" | custom-call | flops 50331648 | bytes 2097152 | tf_op jit(solution)/shard_map/pallas_call | solution.py:286
  44.8 2.9 %collective-permute-start.2 = (f32[24,2048]{1,0:T(8,128)S(1)}, f32[24,2048]{1,0:T(8,128)S(1)}, u32[]{:S(2)}, u32[]{:S(2)}) collective-permute-start(f32[24,2048]{1,0:T(8,128)S(1)} %get-tuple-element.16), channel_id=1, source_target_pairs={{0,1},{1,0},{2,3},{3,2},{4,5},{5,4},{6,7},{7,6},{8,9},{9,8},{10,11... | collective-permute-start | bytes 589832 | tf_op jit(solution)/shard_map/ppermute | solution.py:321
  47.6 0.5 shard_map.75
  48.1 0.0 collective-permute-start.1
  48.1 0.5 shard_map.76
  48.6 0.1 collective-permute-done.2
  48.7 2.2 %collective-permute-start.3 = (bf16[24,2048]{1,0:T(8,128)(2,1)S(1)}, bf16[24,2048]{1,0:T(8,128)(2,1)S(1)}, u32[]{:S(2)}, u32[]{:S(2)}) collective-permute-start(bf16[24,2048]{1,0:T(8,128)(2,1)S(1)} %add_convert_fusion.1), channel_id=1, source_target_pairs={{0,2},{1,3},{2,0},{3,1},{4,6},{5,7},{6,4},{7,5},{8,10},{9,11},{10,... | collective-permute-start | bytes 294920 | tf_op jit(solution)/shard_map/ppermute | solution.py:324
  50.9 0.5 shard_map.74
  51.3 0.0 collective-permute-done.1
  51.3 2.9 %collective-permute-done.3 = bf16[24,2048]{1,0:T(8,128)(2,1)S(1)} collective-permute-done((bf16[24,2048]{1,0:T(8,128)(2,1)S(1)}, bf16[24,2048]{1,0:T(8,128)(2,1)S(1)}, u32[]{:S(2)}, u32[]{:S(2)}) %collective-permute-start.3) | collective-permute-done | bytes 98336 | tf_op jit(solution)/shard_map/ppermute | solution.py:324
  54.3 0.7 %convert_add_fusion = f32[24,2048]{1,0:T(8,128)} fusion(bf16[24,2048]{1,0:T(8,128)(2,1)S(1)} %collective-permute-done.3, f32[24,2048]{1,0:T(8,128)S(1)} %shard_map.74, f32[24,2048]{1,0:T(8,128)S(1)} %collective-permute-done.1), kind=kLoop, calls=%fused_computation.1 | loop fusion | flops 147456 | bytes 688128 | tf_op jit(solution)/shard_map/add | solution.py:328
  (2 shorter events, 0.0 us)
Async XLA Ops:
  0.0 44.0 %slice-start = ((s8[8388608]{0:T(1024)(128)(4,1)}), s8[4194304]{0:T(1024)(128)(4,1)S(1)}, s32[]{:S(2)}) async-start(s8[8388608]{0:T(1024)(128)(4,1)} %bitcast.1), calls=%async_computation.2 | async-start | bytes 8388608
  4.4 4.1 %collective-permute-start = (bf16[32,2,16,256]{3,2,1,0:T(8,128)(2,1)S(1)}, bf16[32,2,16,256]{3,2,1,0:T(8,128)(2,1)S(1)}, u32[]{:S(2)}, u32[]{:S(2)}) collective-permute-start(bf16[32,2,16,256]{3,2,1,0:T(8,128)(2,1)S(1)} %get-tuple-element.14), channel_id=1, source_target_pairs={{0,1},{1,0},{2,3},{3,2},{4,5},{5,4},{6,7},{7,6},{8,9},{9,8},{10,11... | collective-permute-start | bytes 1572872 | tf_op jit(solution)/shard_map/ppermute | solution.py:312
  5.8 38.2 %slice-start.1 = ((s8[8388608]{0:T(1024)(128)(4,1)}), s8[4194304]{0:T(1024)(128)(4,1)S(1)}, s32[]{:S(2)}) async-start(s8[8388608]{0:T(1024)(128)(4,1)} %bitcast.1), calls=%async_computation.3 | async-start | bytes 8388608
  8.4 35.6 %copy-start = (s32[4,24]{1,0:T(4,128)S(1)}, s32[4,24]{1,0:T(4,128)}, u32[]{:S(2)}) copy-start(s32[4,24]{1,0:T(4,128)} %index_ref.1) | copy-start | bytes 1156
  44.8 3.9 %collective-permute-start.2 = (f32[24,2048]{1,0:T(8,128)S(1)}, f32[24,2048]{1,0:T(8,128)S(1)}, u32[]{:S(2)}, u32[]{:S(2)}) collective-permute-start(f32[24,2048]{1,0:T(8,128)S(1)} %get-tuple-element.16), channel_id=1, source_target_pairs={{0,1},{1,0},{2,3},{3,2},{4,5},{5,4},{6,7},{7,6},{8,9},{9,8},{10,11... | collective-permute-start | bytes 589832 | tf_op jit(solution)/shard_map/ppermute | solution.py:321
  48.1 3.3 %collective-permute-start.1 = (f32[24,2048]{1,0:T(8,128)S(1)}, f32[24,2048]{1,0:T(8,128)S(1)}, u32[]{:S(2)}, u32[]{:S(2)}) collective-permute-start(f32[24,2048]{1,0:T(8,128)S(1)} %shard_map.75), channel_id=1, source_target_pairs={{0,1},{1,0},{2,3},{3,2},{4,5},{5,4},{6,7},{7,6},{8,9},{9,8},{10,11... | collective-permute-start | bytes 589832 | tf_op jit(solution)/shard_map/ppermute | solution.py:326
  48.7 5.5 %collective-permute-start.3 = (bf16[24,2048]{1,0:T(8,128)(2,1)S(1)}, bf16[24,2048]{1,0:T(8,128)(2,1)S(1)}, u32[]{:S(2)}, u32[]{:S(2)}) collective-permute-start(bf16[24,2048]{1,0:T(8,128)(2,1)S(1)} %add_convert_fusion.1), channel_id=1, source_target_pairs={{0,2},{1,3},{2,0},{3,1},{4,6},{5,7},{6,4},{7,5},{8,10},{9,11},{10,... | collective-permute-start | bytes 294920 | tf_op jit(solution)/shard_map/ppermute | solution.py:324

commit v6 on v5

--- a/solution.py
+++ b/solution.py
@@ -49,7 +49,7 @@
         others = others + away
 
 
-def accumulate(groups, base, window_ref, order_ref, buffer, weight_ref, factor_ref, high_ref, low_ref, acc_ref, wait):
+def accumulate(groups, base, window_ref, order_ref, buffer, weight_ref, factor_ref, high_ref, low_ref, acc_ref, wait, ready=None):
     per_shot, doubled = buffer.shape[1:]
     rays = weight_ref.shape[0] // 2
 
@@ -68,6 +68,8 @@
         value = lax.dot_general(samples, weight_ref[...], NT, preferred_element_type=F32)
         all_rows = slice(first * per_shot, (first + group) * per_shot)
         high_ref[all_rows], low_ref[all_rows] = split(value)
+        if first == 0 and ready is not None:
+            ready()
         for slot in pending:
             slant(slot, slice(slot * per_shot, (slot + 1) * per_shot))
         pending = range(first, first + group)
@@ -77,13 +79,14 @@
 
 
 def put_sums(acc_ref, out_ref):
-    rays = out_ref.shape[-1]
     for side in range(2):
         for wl in range(WIN_OWN):
             for h in range(2):
-                at = h * 16 + wl * 4
-                block = acc_ref[side * 4 + wl, h * 64 : (h + 1) * 64]
-                out_ref[at : at + 4, side] = block.astype(out_ref.dtype).reshape(4, 16, rays)
+                for quarter in range(4):
+                    at = h * 64 + quarter * 16
+                    block = acc_ref[side * 4 + wl, at : at + 16]
+                    slab = h * 16 + wl * 4 + quarter
+                    out_ref[slab ^ FIRST_SUM[0], side ^ FIRST_SUM[1]] = block.astype(out_ref.dtype)
 
 
 def other_kernel(
@@ -106,7 +109,7 @@
         trace_hbm.at[shot], buffer.at[slot], trace_sems.at[slot]
     )
     for slot in range(shots):
-        load(order_ref[slot], slot).start()
+        load(order_ref[slot], slot).start(priority=1)
 
     small[1].wait()
     small[2].wait()
@@ -156,11 +159,14 @@
     copy.start()
     acc_ref[...] = jnp.zeros_like(acc_ref)
     _, core = beam_position()
-    copy.wait()
-    order_shots(window_ref, order_ref, core)
+
+    def ready():
+        copy.wait()
+        order_shots(window_ref, order_ref, core)
+
     accumulate(
-        (8,), 8, window_ref, order_ref, buffer, weight_ref, factor_ref, high_ref, low_ref,
-        acc_ref, lambda first, count: None,
+        (4, 4), 8, window_ref, order_ref, buffer, weight_ref, factor_ref, high_ref, low_ref,
+        acc_ref, lambda first, count: None, ready,
     )
     put_sums(acc_ref, out_ref)
 
@@ -214,6 +220,8 @@
     return other, mine
 
 
+FIRST_SUM = (20, 1)
+FIRST_SPREAD = 20
 STACK_VMEM = 32 << 20
 MINE_VMEM = 24 << 20
 IMAGE_VMEM = 12 << 20
@@ -250,7 +258,7 @@
     rows = lax.broadcasted_iota(jnp.int32, (rays, 128), 0)
     pick = jnp.transpose((rows == index).astype(F32)).astype(BF16)
     group = lax.broadcasted_iota(jnp.int32, (depths, 512), 1) // P_SIZE % WIN_OWN
-    table = table_ref[...].reshape(512, rays)
+    table = jnp.concatenate([table_ref[i ^ FIRST_SPREAD] for i in range(32)], axis=0)
     waves = lax.dot_general(pick, table, NT, preferred_element_type=F32)
     wave = waves[:depths]
     for wl in range(1, WIN_OWN):
@@ -306,13 +314,17 @@
     scale = (shots * devices * per_shot / (WIN_OWN * beams)) ** -0.5
     partner = [(i, i ^ 1) for i in range(devices)]
     distant = [(i, i ^ 2) for i in range(devices)]
-    same_core = [list(range(core, devices, 2)) for core in range(2)]
+    first = FIRST_SUM[0] * 2 + FIRST_SUM[1]
+    same_core = [[(i ^ first) * 2 + core for i in range(devices // 2)] for core in range(2)]
+    same_beam = [[(i ^ FIRST_SPREAD) * beams + beam for i in range(slabs)] for beam in range(beams)]
 
     other, mine = stack(shot_window, trace_slot, slant_table(scale), ray_phase, traces)
     other = lax.ppermute(other, AXES, partner)
     both = (mine() + other.astype(F32)).astype(BF16).reshape(2 * slabs, 16, rays)
     arrived = lax.all_to_all(both, AXES, 0, 0, axis_index_groups=same_core, tiled=True)
-    table = lax.all_to_all(spread(arrived), "slab", 0, 0, tiled=True)
+    table = lax.all_to_all(
+        spread(arrived), AXES, 0, 0, axis_index_groups=same_beam, tiled=True
+    )
 
     far_other, wave = image_call(first_kernel, depths, chunk, beam_basis, True, ray_index, table)
     call = lambda far, other, wave: image_call(

time: 55.1 us -> 50 us (0.907)
  blocking collectives: 35.3 us -> 30.8 us
  Pallas kernels: 9.15 us -> 8.56 us
    all_to_all x1, blocking collectives: 24 us -> 19.4 us  [body(): lax.all_to_all(both, AXES, 0, 0, axis_index_groups=same_core, tiled=True)]
where the time goes in v6:
time: 50 us; the launch traced here: 49.8 us
  blocking collectives  30.8 us (62%)
  Pallas kernels  8.56 us (17%)
  starting transfers between devices  6.75 us (14%)
  waiting for transfers between devices  2.7 us (5%)
  other arithmetic  0.9 us (2%)
    all_to_all x1, blocking collectives, body(): lax.all_to_all(both, AXES, 0, 0, axis_index_groups=same_core, tiled=True)  19.4 us
    all_to_all x1, blocking collectives, body(): lax.all_to_all(spread(arrived), AXES, 0, 0, axis_index_groups=same_beam,...  11.3 us
    pallas_call x1, Pallas kernels, stack(): pl.pallas_call(other_kernel, out_shape=(shape((32, 2, 16, rays), BF16), s...  4.32 us
    ppermute x1, starting transfers between devices, body(): far_other = lax.ppermute(far_other, AXES, partner)  2.75 us
    ppermute x1, waiting for transfers between devices, body(): far = lax.ppermute(far, AXES, distant)  2.58 us
    ppermute x1, starting transfers between devices, body(): far = lax.ppermute(far, AXES, distant)  2.5 us
    pallas_call x4, Pallas kernels, image_call(): pl.pallas_call(kernel, out_shape=(shape, wave) if wave_out else shape, in...  2.1 us
    pallas_call x1, Pallas kernels, stack(): pl.pallas_call(mine_kernel, out_shape=shape((32, 2, 16, rays), F32), in_s...  2.05 us
  transfers between devices with their start and end apart: 4, of which 2 were waited for; matrix products, arithmetic and copies ran while one was open for 0% of the time, Pallas kernels for 7%

profile of v6, /device:TPU:1, one launch (start us, length us, event | category | flops | bytes accessed | tf_op | source)
XLA Modules:
  0.0 49.8 jit_solution(10473803103387496443)
XLA Ops:
  0.0 0.0 slice-start
  0.0 4.3 %stack_other.1 = (bf16[32,2,16,256]{3,2,1,0:T(8,128)(2,1)S(1)}, bf16[16,128,1024]{2,1,0:T(8,128)(2,1)S(1)}, bf16[512,1024]{1,0:T(8,128)(2,1)S(1)}, bf16[8,256,256]{2,1,0:T(8,128)(2,1)S(1)}) custom-call(s32[16]{0:T(128)} %window_hbm.3, s32[16,128]{1,0:T(8,128)} %slot_hbm.1, bf16[256,128]{1,0:T(8,128)(2,1)} %constant.2.clone.table_hbm, ...), custom_call_target="tpu_custom_call" | custom-call | tf_op jit(solution)/shard_map/stack_other/pallas_call | solution.py:184
  4.3 1.5 %collective-permute-start = (bf16[32,2,16,256]{3,2,1,0:T(8,128)(2,1)S(1)}, bf16[32,2,16,256]{3,2,1,0:T(8,128)(2,1)S(1)}, u32[]{:S(2)}, u32[]{:S(2)}) collective-permute-start(bf16[32,2,16,256]{3,2,1,0:T(8,128)(2,1)S(1)} %get-tuple-element.14), channel_id=1, source_target_pairs={{0,1},{1,0},{2,3},{3,2},{4,5},{5,4},{6,7},{7,6},{8,9},{9,8},{10,11... | collective-permute-start | bytes 1572872 | tf_op jit(solution)/shard_map/ppermute | solution.py:322
  5.8 0.0 slice-start.1
  5.8 2.0 %stack_mine.1 = f32[32,2,16,256]{3,2,1,0:T(8,128)S(1)} custom-call(s32[16]{0:T(128)} %window_hbm.3, bf16[16,128,1024]{2,1,0:T(8,128)(2,1)S(1)} %get-tuple-element.11.buffer, bf16[512,1024]{1,0:T(8,128)(2,1)S(1)} %get-tuple-element.12.weight_ref, bf16[8,256,256]{2,1,0:T(8,128)(2,1)S(1)} %get-tuple-element.13.factor_ref), custom_call_target="tpu_custom_call" | custom-call | flops 2147483648 | bytes 8388608 | tf_op jit(solution)/shard_map/stack_mine/pallas_call | solution.py:210
  7.8 0.0 copy-start
  7.9 0.0 collective-permute-done
  7.9 0.2 add_convert_fusion
  8.1 19.4 %all_to_all.10.arrived_ref = bf16[64,16,256]{2,1,0:T(8,128)(2,1)S(1)} all-to-all(bf16[64,16,256]{2,1,0:T(8,128)(2,1)S(1)} %bitcast.3), channel_id=1, replica_groups={{82,80,86,84,90,88,94,92,66,64,70,68,74,72,78,76,114,112,118,116,122,12..., dimensions={0} | all-to-all | bytes 1048576 | tf_op jit(solution)/shard_map/all_to_all | solution.py:324
  27.5 0.1 spread.1
  27.6 11.3 %all_to_all.11.table_ref = bf16[32,16,256]{2,1,0:T(8,128)(2,1)S(1)} all-to-all(bf16[32,16,256]{2,1,0:T(8,128)(2,1)S(1)} %spread.1), channel_id=1, replica_groups={{80,84,88,92,64,68,72,76,112,116,120,124,96,100,104,108,16,20,24,28,0,4..., dimensions={0} | all-to-all | bytes 524288 | tf_op jit(solution)/shard_map/all_to_all | solution.py:325
  38.9 0.0 slice-done
  38.9 0.0 slice-done.1
  38.9 0.0 copy-done
  39.0 0.7 %shard_map.73 = (f32[24,2048]{1,0:T(8,128)S(1)}, bf16[24,512]{1,0:T(8,128)(2,1)S(1)}) custom-call(s32[4,24]{1,0:T(4,128)S(1)} %copy-done, bf16[32,16,256]{2,1,0:T(8,128)(2,1)S(1)} %all_to_all.11.table_ref, bf16[2,256,8192]{2,1,0:T(8,128)(2,1)S(1)} %bitcast.2), custom_call_target="tpu_custom_call" | custom-call | flops 50331648 | bytes 2097152 | tf_op jit(solution)/shard_map/pallas_call | solution.py:294
  39.7 2.7 %collective-permute-start.2 = (f32[24,2048]{1,0:T(8,128)S(1)}, f32[24,2048]{1,0:T(8,128)S(1)}, u32[]{:S(2)}, u32[]{:S(2)}) collective-permute-start(f32[24,2048]{1,0:T(8,128)S(1)} %get-tuple-element.16), channel_id=1, source_target_pairs={{0,1},{1,0},{2,3},{3,2},{4,5},{5,4},{6,7},{7,6},{8,9},{9,8},{10,11... | collective-permute-start | bytes 589832 | tf_op jit(solution)/shard_map/ppermute | solution.py:333
  42.4 0.5 shard_map.75
  42.9 0.0 collective-permute-start.1
  42.9 0.5 shard_map.76
  43.4 0.1 collective-permute-done.2
  43.5 2.5 %collective-permute-start.3 = (bf16[24,2048]{1,0:T(8,128)(2,1)S(1)}, bf16[24,2048]{1,0:T(8,128)(2,1)S(1)}, u32[]{:S(2)}, u32[]{:S(2)}) collective-permute-start(bf16[24,2048]{1,0:T(8,128)(2,1)S(1)} %add_convert_fusion.1), channel_id=1, source_target_pairs={{0,2},{1,3},{2,0},{3,1},{4,6},{5,7},{6,4},{7,5},{8,10},{9,11},{10,... | collective-permute-start | bytes 294920 | tf_op jit(solution)/shard_map/ppermute | solution.py:336
  46.0 0.5 shard_map.74
  46.5 0.0 collective-permute-done.1
  46.5 2.6 %collective-permute-done.3 = bf16[24,2048]{1,0:T(8,128)(2,1)S(1)} collective-permute-done((bf16[24,2048]{1,0:T(8,128)(2,1)S(1)}, bf16[24,2048]{1,0:T(8,128)(2,1)S(1)}, u32[]{:S(2)}, u32[]{:S(2)}) %collective-permute-start.3) | collective-permute-done | bytes 98336 | tf_op jit(solution)/shard_map/ppermute | solution.py:336
  49.1 0.7 %convert_add_fusion = f32[24,2048]{1,0:T(8,128)} fusion(bf16[24,2048]{1,0:T(8,128)(2,1)S(1)} %collective-permute-done.3, f32[24,2048]{1,0:T(8,128)S(1)} %shard_map.74, f32[24,2048]{1,0:T(8,128)S(1)} %collective-permute-done.1), kind=kLoop, calls=%fused_computation.1 | loop fusion | flops 147456 | bytes 688128 | tf_op jit(solution)/shard_map/add | solution.py:340
  (2 shorter events, 0.0 us)
Async XLA Ops:
  0.0 38.9 %slice-start = ((s8[8388608]{0:T(1024)(128)(4,1)}), s8[4194304]{0:T(1024)(128)(4,1)S(1)}, s32[]{:S(2)}) async-start(s8[8388608]{0:T(1024)(128)(4,1)} %bitcast.1), calls=%async_computation.2 | async-start | bytes 8388608
  4.3 3.5 %collective-permute-start = (bf16[32,2,16,256]{3,2,1,0:T(8,128)(2,1)S(1)}, bf16[32,2,16,256]{3,2,1,0:T(8,128)(2,1)S(1)}, u32[]{:S(2)}, u32[]{:S(2)}) collective-permute-start(bf16[32,2,16,256]{3,2,1,0:T(8,128)(2,1)S(1)} %get-tuple-element.14), channel_id=1, source_target_pairs={{0,1},{1,0},{2,3},{3,2},{4,5},{5,4},{6,7},{7,6},{8,9},{9,8},{10,11... | collective-permute-start | bytes 1572872 | tf_op jit(solution)/shard_map/ppermute | solution.py:322
  5.8 33.2 %slice-start.1 = ((s8[8388608]{0:T(1024)(128)(4,1)}), s8[4194304]{0:T(1024)(128)(4,1)S(1)}, s32[]{:S(2)}) async-start(s8[8388608]{0:T(1024)(128)(4,1)} %bitcast.1), calls=%async_computation.3 | async-start | bytes 8388608
  7.8 31.1 %copy-start = (s32[4,24]{1,0:T(4,128)S(1)}, s32[4,24]{1,0:T(4,128)}, u32[]{:S(2)}) copy-start(s32[4,24]{1,0:T(4,128)} %index_ref.1) | copy-start | bytes 1156
  39.7 3.8 %collective-permute-start.2 = (f32[24,2048]{1,0:T(8,128)S(1)}, f32[24,2048]{1,0:T(8,128)S(1)}, u32[]{:S(2)}, u32[]{:S(2)}) collective-permute-start(f32[24,2048]{1,0:T(8,128)S(1)} %get-tuple-element.16), channel_id=1, source_target_pairs={{0,1},{1,0},{2,3},{3,2},{4,5},{5,4},{6,7},{7,6},{8,9},{9,8},{10,11... | collective-permute-start | bytes 589832 | tf_op jit(solution)/shard_map/ppermute | solution.py:333
  42.9 3.6 %collective-permute-start.1 = (f32[24,2048]{1,0:T(8,128)S(1)}, f32[24,2048]{1,0:T(8,128)S(1)}, u32[]{:S(2)}, u32[]{:S(2)}) collective-permute-start(f32[24,2048]{1,0:T(8,128)S(1)} %shard_map.75), channel_id=1, source_target_pairs={{0,1},{1,0},{2,3},{3,2},{4,5},{5,4},{6,7},{7,6},{8,9},{9,8},{10,11... | collective-permute-start | bytes 589832 | tf_op jit(solution)/shard_map/ppermute | solution.py:338
  43.5 5.5 %collective-permute-start.3 = (bf16[24,2048]{1,0:T(8,128)(2,1)S(1)}, bf16[24,2048]{1,0:T(8,128)(2,1)S(1)}, u32[]{:S(2)}, u32[]{:S(2)}) collective-permute-start(bf16[24,2048]{1,0:T(8,128)(2,1)S(1)} %add_convert_fusion.1), channel_id=1, source_target_pairs={{0,2},{1,3},{2,0},{3,1},{4,6},{5,7},{6,4},{7,5},{8,10},{9,11},{10,... | collective-permute-start | bytes 294920 | tf_op jit(solution)/shard_map/ppermute | solution.py:336

commit v7 on v6

--- a/solution.py
+++ b/solution.py
@@ -50,7 +50,7 @@
 
 
 def accumulate(groups, base, window_ref, order_ref, buffer, weight_ref, factor_ref, high_ref, low_ref, acc_ref, wait, ready=None):
-    per_shot, doubled = buffer.shape[1:]
+    per_shot, _ = buffer.shape[1:]
     rays = weight_ref.shape[0] // 2
 
     def slant(slot, rows):
@@ -64,7 +64,9 @@
     pending, first = [], 0
     for group in groups:
         wait(first, group)
-        samples = buffer[base + first : base + first + group].reshape(group * per_shot, doubled)
+        samples = jnp.concatenate(
+            [buffer[order_ref[base + first + i]] for i in range(group)], axis=0
+        )
         value = lax.dot_general(samples, weight_ref[...], NT, preferred_element_type=F32)
         all_rows = slice(first * per_shot, (first + group) * per_shot)
         high_ref[all_rows], low_ref[all_rows] = split(value)
@@ -102,14 +104,14 @@
     small = [pltpu.make_async_copy(a, b, sems.at[i]) for i, (a, b) in enumerate(pairs)]
     for copy in small:
         copy.start()
+    load = lambda shot: pltpu.make_async_copy(
+        trace_hbm.at[shot], buffer.at[shot], trace_sems.at[shot]
+    )
+    for shot in range(shots):
+        load(shot).start(priority=1)
     acc_ref[...] = jnp.zeros_like(acc_ref)
     small[0].wait()
     order_shots(window_ref, order_ref, core)
-    load = lambda shot, slot: pltpu.make_async_copy(
-        trace_hbm.at[shot], buffer.at[slot], trace_sems.at[slot]
-    )
-    for slot in range(shots):
-        load(order_ref[slot], slot).start(priority=1)
 
     small[1].wait()
     small[2].wait()
@@ -141,7 +143,7 @@
 
     def wait(first, count):
         for slot in range(first, first + count):
-            load(0, slot).wait()
+            load(order_ref[slot]).wait()
 
     accumulate(
         (4, 4), 0, window_ref, order_ref, buffer, weight_ref, factor_ref, high_ref, low_ref,
@@ -160,13 +162,11 @@
     acc_ref[...] = jnp.zeros_like(acc_ref)
     _, core = beam_position()
 
-    def ready():
-        copy.wait()
-        order_shots(window_ref, order_ref, core)
-
+    copy.wait()
+    order_shots(window_ref, order_ref, core)
     accumulate(
         (4, 4), 8, window_ref, order_ref, buffer, weight_ref, factor_ref, high_ref, low_ref,
-        acc_ref, lambda first, count: None, ready,
+        acc_ref, lambda first, count: None,
     )
     put_sums(acc_ref, out_ref)
 
@@ -221,7 +221,7 @@
 
 
 FIRST_SUM = (20, 1)
-FIRST_SPREAD = 20
+FIRST_SPREAD = 21
 STACK_VMEM = 32 << 20
 MINE_VMEM = 24 << 20
 IMAGE_VMEM = 12 << 20

time: 50 us -> 50 us (level)
    pallas_call x1, Pallas kernels: 2.05 us -> 2.59 us  [stack(): pl.pallas_call(mine_kernel, out_shape=shape((32, 2, 16, rays), F32), in_s...]
  transfers between devices with their start and end apart: 4 -> 4, of which waited for: 2 -> 2; matrix products, arithmetic and copies ran while one was open for 0% -> 0% of each run, Pallas kernels for 7% -> 8%
where the time goes in v7:
time: 50 us; the launch traced here: 49.8 us
  blocking collectives  30.5 us (61%)
  Pallas kernels  8.83 us (18%)
  starting transfers between devices  7.05 us (14%)
  waiting for transfers between devices  2.43 us (5%)
  other arithmetic  0.9 us (2%)
    all_to_all x1, blocking collectives, body(): lax.all_to_all(both, AXES, 0, 0, axis_index_groups=same_core, tiled=True)  19.4 us
    all_to_all x1, blocking collectives, body(): lax.all_to_all(spread(arrived), AXES, 0, 0, axis_index_groups=same_beam,...  11.1 us
    pallas_call x1, Pallas kernels, stack(): pl.pallas_call(other_kernel, out_shape=(shape((32, 2, 16, rays), BF16), s...  4.05 us
    ppermute x1, starting transfers between devices, body(): far = lax.ppermute(far, AXES, distant)  2.77 us
    ppermute x1, starting transfers between devices, body(): far_other = lax.ppermute(far_other, AXES, partner)  2.61 us
    pallas_call x1, Pallas kernels, stack(): pl.pallas_call(mine_kernel, out_shape=shape((32, 2, 16, rays), F32), in_s...  2.59 us
    ppermute x1, waiting for transfers between devices, body(): far = lax.ppermute(far, AXES, distant)  2.31 us
    pallas_call x4, Pallas kernels, image_call(): pl.pallas_call(kernel, out_shape=(shape, wave) if wave_out else shape, in...  2.09 us
  transfers between devices with their start and end apart: 4, of which 2 were waited for; matrix products, arithmetic and copies ran while one was open for 0% of the time, Pallas kernels for 8%

profile of v7, /device:TPU:1, one launch (start us, length us, event | category | flops | bytes accessed | tf_op | source)
XLA Modules:
  0.0 49.8 jit_solution(10357842991465930473)
XLA Ops:
  0.0 0.0 slice-start
  0.0 4.1 %stack_other.1 = (bf16[32,2,16,256]{3,2,1,0:T(8,128)(2,1)S(1)}, bf16[16,128,1024]{2,1,0:T(8,128)(2,1)S(1)}, bf16[512,1024]{1,0:T(8,128)(2,1)S(1)}, bf16[8,256,256]{2,1,0:T(8,128)(2,1)S(1)}) custom-call(s32[16]{0:T(128)} %window_hbm.3, s32[16,128]{1,0:T(8,128)} %slot_hbm.1, bf16[256,128]{1,0:T(8,128)(2,1)} %constant.2.clone.table_hbm, ...), custom_call_target="tpu_custom_call" | custom-call | tf_op jit(solution)/shard_map/stack_other/pallas_call | solution.py:184
  4.1 1.6 %collective-permute-start = (bf16[32,2,16,256]{3,2,1,0:T(8,128)(2,1)S(1)}, bf16[32,2,16,256]{3,2,1,0:T(8,128)(2,1)S(1)}, u32[]{:S(2)}, u32[]{:S(2)}) collective-permute-start(bf16[32,2,16,256]{3,2,1,0:T(8,128)(2,1)S(1)} %get-tuple-element.14), channel_id=1, source_target_pairs={{0,1},{1,0},{2,3},{3,2},{4,5},{5,4},{6,7},{7,6},{8,9},{9,8},{10,11... | collective-permute-start | bytes 1572872 | tf_op jit(solution)/shard_map/ppermute | solution.py:322
  5.7 0.0 slice-start.1
  5.7 2.6 %stack_mine.1 = f32[32,2,16,256]{3,2,1,0:T(8,128)S(1)} custom-call(s32[16]{0:T(128)} %window_hbm.3, bf16[16,128,1024]{2,1,0:T(8,128)(2,1)S(1)} %get-tuple-element.11.buffer, bf16[512,1024]{1,0:T(8,128)(2,1)S(1)} %get-tuple-element.12.weight_ref, bf16[8,256,256]{2,1,0:T(8,128)(2,1)S(1)} %get-tuple-element.13.factor_ref), custom_call_target="tpu_custom_call" | custom-call | flops 2147483648 | bytes 8388608 | tf_op jit(solution)/shard_map/stack_mine/pallas_call | solution.py:210
  8.3 0.0 copy-start
  8.3 0.0 collective-permute-done
  8.3 0.2 add_convert_fusion
  8.5 19.4 %all_to_all.10.arrived_ref = bf16[64,16,256]{2,1,0:T(8,128)(2,1)S(1)} all-to-all(bf16[64,16,256]{2,1,0:T(8,128)(2,1)S(1)} %bitcast.3), channel_id=1, replica_groups={{82,80,86,84,90,88,94,92,66,64,70,68,74,72,78,76,114,112,118,116,122,12..., dimensions={0} | all-to-all | bytes 1048576 | tf_op jit(solution)/shard_map/all_to_all | solution.py:324
  27.9 0.1 spread.1
  28.0 11.1 %all_to_all.11.table_ref = bf16[32,16,256]{2,1,0:T(8,128)(2,1)S(1)} all-to-all(bf16[32,16,256]{2,1,0:T(8,128)(2,1)S(1)} %spread.1), channel_id=1, replica_groups={{84,80,92,88,68,64,76,72,116,112,124,120,100,96,108,104,20,16,28,24,4,0..., dimensions={0} | all-to-all | bytes 524288 | tf_op jit(solution)/shard_map/all_to_all | solution.py:325
  39.1 0.0 slice-done
  39.1 0.0 slice-done.1
  39.1 0.0 copy-done
  39.1 0.7 %shard_map.73 = (f32[24,2048]{1,0:T(8,128)S(1)}, bf16[24,512]{1,0:T(8,128)(2,1)S(1)}) custom-call(s32[4,24]{1,0:T(4,128)S(1)} %copy-done, bf16[32,16,256]{2,1,0:T(8,128)(2,1)S(1)} %all_to_all.11.table_ref, bf16[2,256,8192]{2,1,0:T(8,128)(2,1)S(1)} %bitcast.2), custom_call_target="tpu_custom_call" | custom-call | flops 50331648 | bytes 2097152 | tf_op jit(solution)/shard_map/pallas_call | solution.py:294
  39.9 2.6 %collective-permute-start.2 = (f32[24,2048]{1,0:T(8,128)S(1)}, f32[24,2048]{1,0:T(8,128)S(1)}, u32[]{:S(2)}, u32[]{:S(2)}) collective-permute-start(f32[24,2048]{1,0:T(8,128)S(1)} %get-tuple-element.16), channel_id=1, source_target_pairs={{0,1},{1,0},{2,3},{3,2},{4,5},{5,4},{6,7},{7,6},{8,9},{9,8},{10,11... | collective-permute-start | bytes 589832 | tf_op jit(solution)/shard_map/ppermute | solution.py:333
  42.5 0.5 shard_map.75
  42.9 0.0 collective-permute-start.1
  43.0 0.5 shard_map.76
  43.4 0.1 collective-permute-done.2
  43.6 2.8 %collective-permute-start.3 = (bf16[24,2048]{1,0:T(8,128)(2,1)S(1)}, bf16[24,2048]{1,0:T(8,128)(2,1)S(1)}, u32[]{:S(2)}, u32[]{:S(2)}) collective-permute-start(bf16[24,2048]{1,0:T(8,128)(2,1)S(1)} %add_convert_fusion.1), channel_id=1, source_target_pairs={{0,2},{1,3},{2,0},{3,1},{4,6},{5,7},{6,4},{7,5},{8,10},{9,11},{10,... | collective-permute-start | bytes 294920 | tf_op jit(solution)/shard_map/ppermute | solution.py:336
  46.3 0.5 shard_map.74
  46.8 0.0 collective-permute-done.1
  46.8 2.3 %collective-permute-done.3 = bf16[24,2048]{1,0:T(8,128)(2,1)S(1)} collective-permute-done((bf16[24,2048]{1,0:T(8,128)(2,1)S(1)}, bf16[24,2048]{1,0:T(8,128)(2,1)S(1)}, u32[]{:S(2)}, u32[]{:S(2)}) %collective-permute-start.3) | collective-permute-done | bytes 98336 | tf_op jit(solution)/shard_map/ppermute | solution.py:336
  49.1 0.7 %convert_add_fusion = f32[24,2048]{1,0:T(8,128)} fusion(bf16[24,2048]{1,0:T(8,128)(2,1)S(1)} %collective-permute-done.3, f32[24,2048]{1,0:T(8,128)S(1)} %shard_map.74, f32[24,2048]{1,0:T(8,128)S(1)} %collective-permute-done.1), kind=kLoop, calls=%fused_computation.1 | loop fusion | flops 147456 | bytes 688128 | tf_op jit(solution)/shard_map/add | solution.py:340
  (2 shorter events, 0.0 us)
Async XLA Ops:
  0.0 39.1 %slice-start = ((s8[8388608]{0:T(1024)(128)(4,1)}), s8[4194304]{0:T(1024)(128)(4,1)S(1)}, s32[]{:S(2)}) async-start(s8[8388608]{0:T(1024)(128)(4,1)} %bitcast.1), calls=%async_computation.2 | async-start | bytes 8388608
  4.1 4.2 %collective-permute-start = (bf16[32,2,16,256]{3,2,1,0:T(8,128)(2,1)S(1)}, bf16[32,2,16,256]{3,2,1,0:T(8,128)(2,1)S(1)}, u32[]{:S(2)}, u32[]{:S(2)}) collective-permute-start(bf16[32,2,16,256]{3,2,1,0:T(8,128)(2,1)S(1)} %get-tuple-element.14), channel_id=1, source_target_pairs={{0,1},{1,0},{2,3},{3,2},{4,5},{5,4},{6,7},{7,6},{8,9},{9,8},{10,11... | collective-permute-start | bytes 1572872 | tf_op jit(solution)/shard_map/ppermute | solution.py:322
  5.7 33.4 %slice-start.1 = ((s8[8388608]{0:T(1024)(128)(4,1)}), s8[4194304]{0:T(1024)(128)(4,1)S(1)}, s32[]{:S(2)}) async-start(s8[8388608]{0:T(1024)(128)(4,1)} %bitcast.1), calls=%async_computation.3 | async-start | bytes 8388608
  8.3 30.8 %copy-start = (s32[4,24]{1,0:T(4,128)S(1)}, s32[4,24]{1,0:T(4,128)}, u32[]{:S(2)}) copy-start(s32[4,24]{1,0:T(4,128)} %index_ref.1) | copy-start | bytes 1156
  39.9 3.7 %collective-permute-start.2 = (f32[24,2048]{1,0:T(8,128)S(1)}, f32[24,2048]{1,0:T(8,128)S(1)}, u32[]{:S(2)}, u32[]{:S(2)}) collective-permute-start(f32[24,2048]{1,0:T(8,128)S(1)} %get-tuple-element.16), channel_id=1, source_target_pairs={{0,1},{1,0},{2,3},{3,2},{4,5},{5,4},{6,7},{7,6},{8,9},{9,8},{10,11... | collective-permute-start | bytes 589832 | tf_op jit(solution)/shard_map/ppermute | solution.py:333
  42.9 3.9 %collective-permute-start.1 = (f32[24,2048]{1,0:T(8,128)S(1)}, f32[24,2048]{1,0:T(8,128)S(1)}, u32[]{:S(2)}, u32[]{:S(2)}) collective-permute-start(f32[24,2048]{1,0:T(8,128)S(1)} %shard_map.75), channel_id=1, source_target_pairs={{0,1},{1,0},{2,3},{3,2},{4,5},{5,4},{6,7},{7,6},{8,9},{9,8},{10,11... | collective-permute-start | bytes 589832 | tf_op jit(solution)/shard_map/ppermute | solution.py:338
  43.6 5.5 %collective-permute-start.3 = (bf16[24,2048]{1,0:T(8,128)(2,1)S(1)}, bf16[24,2048]{1,0:T(8,128)(2,1)S(1)}, u32[]{:S(2)}, u32[]{:S(2)}) collective-permute-start(bf16[24,2048]{1,0:T(8,128)(2,1)S(1)} %add_convert_fusion.1), channel_id=1, source_target_pairs={{0,2},{1,3},{2,0},{3,1},{4,6},{5,7},{6,4},{7,5},{8,10},{9,11},{10,... | collective-permute-start | bytes 294920 | tf_op jit(solution)/shard_map/ppermute | solution.py:336
